TPU v7x, 32 devices: a whole 2x2x4 slice. The times are simulated.
32 devices in a mesh: fsdp: 8 (over y, x, core), seq: 4 (over z).
Axes of the slice: x: 2, y: 2, z: 4, core: 2. Of those that a mesh axis runs over, the one named last changes fastest.
Arguments:
- tokens: bfloat16 [8, 2048, 768], P('fsdp', 'seq'), may hold values from -6 to 6
- cotangent: bfloat16 [8, 2048, 768], P('fsdp', 'seq'), may hold values from -6 to 6
- w_qkv: bfloat16 [768, 2304], P(('fsdp', 'seq')), may hold values from -0.3125 to 0.3125
- b_qkv: bfloat16 [2304], P(('fsdp', 'seq')), may hold values from -1.796875 to 1.796875
- w_out: bfloat16 [768, 768], P(('fsdp', 'seq')), may hold values from -0.875 to 0.875
- b_out: bfloat16 [768], P(('fsdp', 'seq')), may hold values from -1.796875 to 1.796875
- w_up: bfloat16 [768, 3072], P(('fsdp', 'seq')), may hold values from -0.21875 to 0.21875
- b_up: bfloat16 [3072], P(('fsdp', 'seq')), may hold values from -1.796875 to 1.796875
- w_down: bfloat16 [3072, 768], P(('fsdp', 'seq')), may hold values from -0.109375 to 0.109375
- b_down: bfloat16 [768], P(('fsdp', 'seq')), may hold values from -1.796875 to 1.796875
- gain_attn: bfloat16 [768], P(('fsdp', 'seq')), may hold values from 0.099609375 to 1.8984375
- shift_attn: bfloat16 [768], P(('fsdp', 'seq')), may hold values from -1.796875 to 1.796875
- gain_mlp: bfloat16 [768], P(('fsdp', 'seq')), may hold values from 0.099609375 to 1.8984375
- shift_mlp: bfloat16 [768], P(('fsdp', 'seq')), may hold values from -1.796875 to 1.796875
Outputs:
- block_out: bfloat16 [8, 2048, 768], P('fsdp', 'seq')
- grad_tokens: bfloat16 [8, 2048, 768], P('fsdp', 'seq')
- grad_w_qkv: float32 [768, 2304], P(('fsdp', 'seq'))
- grad_b_qkv: float32 [2304], P(('fsdp', 'seq'))
- grad_w_out: float32 [768, 768], P(('fsdp', 'seq'))
- grad_b_out: float32 [768], P(('fsdp', 'seq'))
- grad_w_up: float32 [768, 3072], P(('fsdp', 'seq'))
- grad_b_up: float32 [3072], P(('fsdp', 'seq'))
- grad_w_down: float32 [3072, 768], P(('fsdp', 'seq'))
- grad_b_down: float32 [768], P(('fsdp', 'seq'))
- grad_gain_attn: float32 [768], P(('fsdp', 'seq'))
- grad_shift_attn: float32 [768], P(('fsdp', 'seq'))
- grad_gain_mlp: float32 [768], P(('fsdp', 'seq'))
- grad_shift_mlp: float32 [768], P(('fsdp', 'seq'))
All inputs are finite; a program needn't handle non-finite values.
Results may differ from a plain program's by a relative error of at most 0.012.
The roundings to bfloat16 on the way count: a program that leaves them out, or rounds other values in their place, can miss the bound.
Values may be sent and summed in bfloat16 or wider, within the bound.
No kernel may reach another device: no remote copies, remote signals or barrier semaphores. Data moves between devices by JAX's collectives and lax.ppermute only.
A program may use at most 192 MiB of HBM per device.

v0:
```python
import math

import jax
import jax.numpy as jnp
from jax import lax
from jax.sharding import PartitionSpec as P

HEAD = 64
ROT = 16


eps = 1e-05
mask_fill = -1e30


def for_sending(shard):

    def short(part):
        return part.astype(jnp.bfloat16) if part.dtype == jnp.float32 else part

    return jax.tree.map(short, shard)


def layer_norm(inputs, gain_vec, shift_vec):
    row_mean = jnp.mean(inputs, axis=-1, keepdims=True)
    centred = inputs - row_mean
    row_var = jnp.mean(centred * centred, axis=-1, keepdims=True)
    return centred * lax.rsqrt(row_var + eps) * gain_vec + shift_vec


def rotary_tables(positions):
    half_rot = ROT // 2
    freq_index = jnp.arange(half_rot, dtype=jnp.int32).astype(jnp.float32)
    inv_freq = jnp.exp(freq_index * (-2.0 * math.log(10000.0) / ROT))
    angles = positions.astype(jnp.float32)[:, None] * inv_freq[None, :]
    return (jnp.cos(angles), jnp.sin(angles))


def rotate(heads_arr, cosine_tab, sine_tab):
    half_rot = ROT // 2
    first_half = heads_arr[..., :half_rot]
    second_half = heads_arr[..., half_rot:ROT]
    rest_part = heads_arr[..., ROT:]
    cos_wide = cosine_tab[:, None, :]
    sin_wide = sine_tab[:, None, :]
    return jnp.concatenate(
        [
            first_half * cos_wide - second_half * sin_wide,
            second_half * cos_wide + first_half * sin_wide,
            rest_part,
        ],
        axis=-1,
    )


def gelu_exact(inputs):
    return jax.nn.gelu(inputs, approximate=False)


def block_scores(seq_qkv, row_begin, finish, score_scale):
    local_heads = seq_qkv.shape[2] // HEAD
    block_rows = finish - row_begin
    queries = seq_qkv[row_begin:finish, 0].reshape(block_rows, local_heads, HEAD)
    key_blk = seq_qkv[:finish, 1].reshape(finish, local_heads, HEAD)
    value_blk = seq_qkv[:finish, 2].reshape(finish, local_heads, HEAD)
    scores = (
        jnp.einsum("qhd,khd->hqk", queries, key_blk, preferred_element_type=jnp.float32)
        * score_scale
    )
    query_pos = row_begin + jnp.arange(block_rows, dtype=jnp.int32)
    allowed = jnp.arange(finish, dtype=jnp.int32)[None, :] <= query_pos[:, None]
    masked = jnp.where(allowed[None], scores, mask_fill)
    return (queries, key_blk, value_blk, masked)


def attend_forward(seq_qkv, score_scale):
    full_len = seq_qkv.shape[0]
    local_heads = seq_qkv.shape[2] // HEAD
    block_rows = min(512, full_len)
    out_parts = []
    lse_parts = []
    for block_idx in range(full_len // block_rows):
        row_begin = block_idx * block_rows
        finish = row_begin + block_rows
        queries, key_blk, value_blk, masked = block_scores(seq_qkv, row_begin, finish, score_scale)
        row_max = jnp.max(masked, axis=-1, keepdims=True)
        exponent = jnp.exp(masked - row_max)
        row_total = jnp.sum(exponent, axis=-1, keepdims=True)
        prob_low = (exponent / row_total).astype(jnp.bfloat16)
        out_blk = jnp.einsum(
            "hqk,khd->qhd", prob_low, value_blk, preferred_element_type=jnp.float32
        )
        out_parts.append(out_blk.reshape(block_rows, local_heads * HEAD))
        lse_parts.append((row_max + jnp.log(row_total))[..., 0])
    mixed_seq = jnp.concatenate(out_parts, axis=0).astype(jnp.bfloat16)
    return (mixed_seq, jnp.concatenate(lse_parts, axis=1))


def attend_backward(seq_qkv, seq_grad, seq_lse, score_scale):
    full_len = seq_qkv.shape[0]
    local_heads = seq_qkv.shape[2] // HEAD
    block_rows = min(512, full_len)
    query_parts = []
    grad_key = jnp.zeros((full_len, local_heads, HEAD), jnp.float32)
    grad_value = jnp.zeros((full_len, local_heads, HEAD), jnp.float32)
    for block_idx in range(full_len // block_rows):
        row_begin = block_idx * block_rows
        finish = row_begin + block_rows
        queries, key_blk, value_blk, masked = block_scores(seq_qkv, row_begin, finish, score_scale)
        prob_blk = jnp.exp(masked - seq_lse[:, row_begin:finish, None])
        prob_low = prob_blk.astype(jnp.bfloat16)
        grad_blk = seq_grad[row_begin:finish].reshape(block_rows, local_heads, HEAD)
        grad_prob = jnp.einsum(
            "qhd,khd->hqk", grad_blk, value_blk, preferred_element_type=jnp.float32
        )
        delta_row = jnp.sum(prob_blk * grad_prob, axis=-1, keepdims=True)
        grad_score = (prob_blk * (grad_prob - delta_row)).astype(jnp.bfloat16)
        query_parts.append(
            jnp.einsum("hqk,khd->qhd", grad_score, key_blk, preferred_element_type=jnp.float32)
            * score_scale
        )
        grad_key = grad_key.at[:finish].add(
            jnp.einsum("hqk,qhd->khd", grad_score, queries, preferred_element_type=jnp.float32)
            * score_scale
        )
        grad_value = grad_value.at[:finish].add(
            jnp.einsum("hqk,qhd->khd", prob_low, grad_blk, preferred_element_type=jnp.float32)
        )
    grad_query = jnp.concatenate(query_parts, axis=0)
    stacked = jnp.stack([grad_query, grad_key, grad_value], axis=1)
    return stacked.reshape(full_len, 3, local_heads * HEAD).astype(jnp.bfloat16)


def body(
    tokens,
    cotangent,
    w_qkv,
    b_qkv,
    w_out,
    b_out,
    w_up,
    b_up,
    w_down,
    b_down,
    gain_attn,
    shift_attn,
    gain_mlp,
    shift_mlp,
):
    seq_count, local_len, model_width = tokens.shape
    row_count = seq_count * local_len
    seq_rank = lax.axis_index("seq")
    fetched = (
        lax.all_gather(w_qkv, ("fsdp", "seq"), axis=0, tiled=True),
        lax.all_gather(b_qkv, ("fsdp", "seq"), axis=0, tiled=True),
        lax.all_gather(w_out, ("fsdp", "seq"), axis=0, tiled=True),
        lax.all_gather(b_out, ("fsdp", "seq"), axis=0, tiled=True),
        lax.all_gather(w_up, ("fsdp", "seq"), axis=0, tiled=True),
        lax.all_gather(b_up, ("fsdp", "seq"), axis=0, tiled=True),
        lax.all_gather(w_down, ("fsdp", "seq"), axis=0, tiled=True),
        lax.all_gather(b_down, ("fsdp", "seq"), axis=0, tiled=True),
        lax.all_gather(gain_attn, ("fsdp", "seq"), axis=0, tiled=True),
        lax.all_gather(shift_attn, ("fsdp", "seq"), axis=0, tiled=True),
        lax.all_gather(gain_mlp, ("fsdp", "seq"), axis=0, tiled=True),
        lax.all_gather(shift_mlp, ("fsdp", "seq"), axis=0, tiled=True),
    )
    (
        full_qkv,
        bias_qkv,
        full_out,
        bias_out,
        full_up,
        bias_up,
        full_down,
        bias_down,
        gain_one,
        shift_one,
        gain_two,
        shift_two,
    ) = fetched
    x_flat = tokens.reshape(row_count, model_width).astype(jnp.float32)
    norm_one, back_one = jax.vjp(
        layer_norm, x_flat, gain_one.astype(jnp.float32), shift_one.astype(jnp.float32)
    )
    norm_two, back_two = jax.vjp(
        layer_norm, x_flat, gain_two.astype(jnp.float32), shift_two.astype(jnp.float32)
    )
    normed_one = norm_one.astype(jnp.bfloat16)
    normed_two = norm_two.astype(jnp.bfloat16)
    projected = jnp.dot(normed_one, full_qkv, preferred_element_type=jnp.float32) + bias_qkv.astype(
        jnp.float32
    )
    positions = seq_rank * local_len + jnp.arange(local_len, dtype=jnp.int32)
    cosine_tab, sine_tab = rotary_tables(positions)

    def turn_all(proj_rows):
        parts = proj_rows.reshape(seq_count, local_len, 3, model_width // HEAD, HEAD)
        query_rot = rotate(parts[:, :, 0], cosine_tab, sine_tab)
        key_rot = rotate(parts[:, :, 1], cosine_tab, sine_tab)
        stacked = jnp.stack([query_rot, key_rot, parts[:, :, 2]], axis=2)
        return stacked.reshape(seq_count, local_len, 3, model_width)

    turned, turn_back = jax.vjp(turn_all, projected)
    turned_low = turned.astype(jnp.bfloat16)
    by_head = lax.all_to_all(turned_low, "seq", split_axis=3, concat_axis=1, tiled=True)
    score_scale = HEAD ** (-0.5)

    def forward_one(seq_qkv):
        return attend_forward(seq_qkv, score_scale)

    mixed_heads, lse_all = lax.map(forward_one, by_head)
    mixed_tok = jax.tree.map(
        lambda part, own: part.astype(own.dtype),
        lax.all_to_all(for_sending(mixed_heads), "seq", split_axis=1, concat_axis=2, tiled=True),
        mixed_heads,
    )
    mixed_flat = mixed_tok.reshape(row_count, model_width)
    attn_out = jnp.dot(mixed_flat, full_out, preferred_element_type=jnp.float32) + bias_out.astype(
        jnp.float32
    )
    hidden_pre = jnp.dot(normed_two, full_up, preferred_element_type=jnp.float32) + bias_up.astype(
        jnp.float32
    )
    hidden_act, gelu_back = jax.vjp(gelu_exact, hidden_pre)
    hidden_low = hidden_act.astype(jnp.bfloat16)
    mlp_out = jnp.dot(hidden_low, full_down, preferred_element_type=jnp.float32) + bias_down.astype(
        jnp.float32
    )
    block_out = (x_flat + attn_out + mlp_out).astype(jnp.bfloat16).reshape(tokens.shape)
    back_qkv, back_out, back_up, back_down = (
        lax.all_gather(w_qkv, ("fsdp", "seq"), axis=0, tiled=True),
        lax.all_gather(w_out, ("fsdp", "seq"), axis=0, tiled=True),
        lax.all_gather(w_up, ("fsdp", "seq"), axis=0, tiled=True),
        lax.all_gather(w_down, ("fsdp", "seq"), axis=0, tiled=True),
    )
    grad_rows = cotangent.reshape(row_count, model_width)
    grad_float = grad_rows.astype(jnp.float32)
    sum_out = jnp.sum(grad_float, axis=0)
    grad_hidden = jnp.einsum("nd,fd->nf", grad_rows, back_down, preferred_element_type=jnp.float32)
    grad_pre = gelu_back(grad_hidden)[0].astype(jnp.bfloat16)
    sum_up = jnp.sum(grad_pre.astype(jnp.float32), axis=0)
    grad_norm_two = jnp.einsum("nf,df->nd", grad_pre, back_up, preferred_element_type=jnp.float32)
    grad_mixed = jnp.einsum("ne,de->nd", grad_rows, back_out, preferred_element_type=jnp.float32)
    grad_mixed = grad_mixed.astype(jnp.bfloat16).reshape(seq_count, local_len, model_width)
    grad_heads = lax.all_to_all(grad_mixed, "seq", split_axis=2, concat_axis=1, tiled=True)

    def backward_one(packed):
        seq_qkv, seq_grad, seq_lse = packed
        return attend_backward(seq_qkv, seq_grad, seq_lse, score_scale)

    grad_turned_heads = lax.map(backward_one, (by_head, grad_heads, lse_all))
    grad_turned = lax.all_to_all(grad_turned_heads, "seq", split_axis=1, concat_axis=3, tiled=True)
    grad_proj = turn_back(grad_turned.astype(jnp.float32))[0].astype(jnp.bfloat16)
    sum_qkv = jnp.sum(grad_proj.astype(jnp.float32), axis=0)
    grad_norm_one = jnp.einsum("ne,de->nd", grad_proj, back_qkv, preferred_element_type=jnp.float32)
    input_part_one, grad_gain_one, grad_shift_one = back_one(grad_norm_one)
    input_part_two, grad_gain_two, grad_shift_two = back_two(grad_norm_two)
    grad_tokens = (
        (grad_float + input_part_one + input_part_two).astype(jnp.bfloat16).reshape(tokens.shape)
    )
    grad_wdown = jnp.einsum("nf,nd->fd", hidden_low, grad_rows, preferred_element_type=jnp.float32)
    grad_wup = jnp.einsum("nd,nf->df", normed_two, grad_pre, preferred_element_type=jnp.float32)
    grad_wout = jnp.einsum("nd,ne->de", mixed_flat, grad_rows, preferred_element_type=jnp.float32)
    grad_wqkv = jnp.einsum("nd,ne->de", normed_one, grad_proj, preferred_element_type=jnp.float32)
    summed = (
        lax.psum_scatter(grad_wqkv, ("fsdp", "seq"), scatter_dimension=0, tiled=True),
        lax.psum_scatter(sum_qkv, ("fsdp", "seq"), scatter_dimension=0, tiled=True),
        lax.psum_scatter(grad_wout, ("fsdp", "seq"), scatter_dimension=0, tiled=True),
        lax.psum_scatter(sum_out, ("fsdp", "seq"), scatter_dimension=0, tiled=True),
        lax.psum_scatter(grad_wup, ("fsdp", "seq"), scatter_dimension=0, tiled=True),
        lax.psum_scatter(sum_up, ("fsdp", "seq"), scatter_dimension=0, tiled=True),
        lax.psum_scatter(grad_wdown, ("fsdp", "seq"), scatter_dimension=0, tiled=True),
        lax.psum_scatter(sum_out, ("fsdp", "seq"), scatter_dimension=0, tiled=True),
        lax.psum_scatter(grad_gain_one, ("fsdp", "seq"), scatter_dimension=0, tiled=True),
        lax.psum_scatter(grad_shift_one, ("fsdp", "seq"), scatter_dimension=0, tiled=True),
        lax.psum_scatter(grad_gain_two, ("fsdp", "seq"), scatter_dimension=0, tiled=True),
        lax.psum_scatter(grad_shift_two, ("fsdp", "seq"), scatter_dimension=0, tiled=True),
    )
    return (
        block_out,
        grad_tokens,
        summed[0],
        summed[1],
        summed[2],
        summed[3],
        summed[4],
        summed[5],
        summed[6],
        summed[7],
        summed[8],
        summed[9],
        summed[10],
        summed[11],
    )


def solution(mesh):
    return jax.shard_map(
        body,
        mesh=mesh,
        in_specs=(
            P("fsdp", "seq", None),
            P("fsdp", "seq", None),
            P(("fsdp", "seq"), None),
            P(("fsdp", "seq")),
            P(("fsdp", "seq"), None),
            P(("fsdp", "seq")),
            P(("fsdp", "seq"), None),
            P(("fsdp", "seq")),
            P(("fsdp", "seq"), None),
            P(("fsdp", "seq")),
            P(("fsdp", "seq")),
            P(("fsdp", "seq")),
            P(("fsdp", "seq")),
            P(("fsdp", "seq")),
        ),
        out_specs=(
            P("fsdp", "seq", None),
            P("fsdp", "seq", None),
            P(("fsdp", "seq"), None),
            P(("fsdp", "seq")),
            P(("fsdp", "seq"), None),
            P(("fsdp", "seq")),
            P(("fsdp", "seq"), None),
            P(("fsdp", "seq")),
            P(("fsdp", "seq"), None),
            P(("fsdp", "seq")),
            P(("fsdp", "seq")),
            P(("fsdp", "seq")),
            P(("fsdp", "seq")),
            P(("fsdp", "seq")),
        ),
        check_vma=False,
    )
```

profile of v0, /device:TPU:0, one launch (start us, length us, event | category | flops | bytes accessed | tf_op | source)
XLA Modules:
  0.0 880.0 jit_solution(89257930912281306)
XLA Ops:
  16.1 42.9 %all-reduce.27 = (bf16[768]{0:T(1024)(128)(2,1)}, bf16[768]{0:T(1024)(128)(2,1)}, bf16[3072]{0:T(1024)(128)(2,1)}, bf16[2304]{0:T(1024)(128)(2,1)S(1)}, bf16[768...) all-reduce(bf16[768]{0:T(1024)(128)(2,1)S(1)} %dynamic-update-slice, ...), channel_id=1, replica_groups=mesh['fsdp'=8,'seq'=4] {'fsdp','seq'}, use_global_device_ids=true, to_apply=%add.16 | all-reduce | flops 9984 | bytes 39936
  62.6 11.2 %all-gather.5.cloned.1.call-done = bf16[768,2304]{1,0:T(8,128)(2,1)} async-done(((bf16[24,2304]{1,0:T(8,128)(2,1)}), bf16[768,2304]{1,0:T(8,128)(2,1)}) %all-gather.5.cloned.1.call-update) | async-done | bytes 3538960 | tf_op jit(solution)/shard_map/all_gather | solution.py:154
  73.8 6.6 convolution_add_fusion
  80.3 6.1 copy.91
  87.9 2.2 slice_bitcast_fusion.3
  90.8 3.7 copy.92
  94.5 3.7 all-to-all-start
  103.7 84.8 %all-to-all-done = bf16[1,512,3,768]{1,2,0,3:T(4,128)(2,1)S(1)} async-done(((bf16[1,512,3,768]{1,2,0,3:T(4,128)(2,1)}), bf16[1,512,3,768]{1,2,0,3:T(4,128)(2,1)S(1)}, u32[]{:S(2)}, u32[]{:S(2)}) %all-to-all-start) | async-done | bytes 2359328 | tf_op jit(solution)/shard_map/all_to_all | solution.py:205
  189.1 3.2 copy.94
  192.3 4.8 squeeze.101
  203.8 2.3 fusion.107
  206.1 2.0 fusion.152
  209.6 2.1 copy-done.1
  211.7 3.3 fusion.101
  215.1 2.6 fusion.151
  219.7 2.6 copy-done
  222.3 3.1 fusion.108
  228.7 5.9 copy.96
  235.1 13.7 %reduce.24 = bf16[2048,192]{1,0:T(8,128)(2,1)} reduce(bf16[2048,1,192]{2,1,0:T(2,128)(2,1)} %bitcast.280, bf16[]{:T(256)} %broadcast.539), dimensions={1}, to_apply=%bitcast.201.reduce_sub_computation | reduce | bytes 1572866
  248.8 3.9 reshape.893
  252.7 4.2 all-to-all-start.1
  257.0 20.4 %all-to-all-done.1 = bf16[4,2,49152]{2,1,0:T(2,128)(2,1)} async-done(((bf16[4,2,49152]{2,1,0:T(2,128)(2,1)}), bf16[4,2,49152]{2,1,0:T(2,128)(2,1)}, u32[]{:S(2)}, u32[]{:S(2)}) %all-to-all-start.1) | async-done | bytes 786464 | tf_op jit(solution)/shard_map/all_to_all | solution.py:214
  277.5 4.1 reshape.894
  281.6 5.7 copy.97
  287.3 3.0 all_to_all.44
  292.5 3.4 fusion.120
  296.0 20.3 %multiply_convert_fusion.3 = (bf16[512,3072]{1,0:T(8,128)(2,1)}, f32[512,3072]{1,0:T(8,128)}, f32[512,3072]{1,0:T(8,128)}) fusion(f32[3072]{0:T(1024)S(1)} %convert_element_type.201, bf16[768,3072]{1,0:T(8,128)(2,1)} %all-gather.9.cloned.1.call-done, bf16[1,512,768]{2,1,0:T(8,128)(2,1)} %param.34, f32[768]{0:T(1024)S(1)} %convert_element_type.199, ...), kind=kOutput, calls=%fused_computation.25 | convolution fusion | flops 2522087424 | bytes 21256192 | tf_op jit(solution)/shard_map/dot_general | solution.py:221
  316.4 11.5 %convert_reduce_fusion = (f32[3072]{0:T(1024)}, bf16[512,3072]{1,0:T(8,128)(2,1)S(1)}) fusion(f32[512,3072]{1,0:T(8,128)} %get-tuple-element.221, bf16[3072,768]{1,0:T(8,128)(2,1)} %all-gather.11.cloned.1.call-done, bf16[1,512,768]{2,1,0:T(8,128)(2,1)} %param.35, f32[512,3072]{1,0:T(8,128)} %get-tuple-element.263, f32[3072]{0:T(1024)S(1)} %convert_element_type.201), kind=kOutput, calls=%fused_computation.19 | convolution fusion | flops 2442654720 | bytes 21258240 | tf_op jit(solution)/shard_map/nd,fd->nf/dot_general | solution.py:239
  329.5 5.5 fusion.136
  335.1 3.2 fusion.84
  338.3 4.9 copy.99
  343.3 7.3 reduce.25
  350.6 2.4 reshape.895
  352.9 30.2 %all_to_all.54 = bf16[4,2,49152]{2,1,0:T(2,128)(2,1)} all-to-all(bf16[4,2,49152]{2,1,0:T(2,128)(2,1)} %reshape.895), channel_id=1, replica_groups=mesh['fsdp'=8,'seq'=4] {'seq'}, dimensions={0} | all-to-all | bytes 1572864 | tf_op jit(solution)/shard_map/all_to_all | solution.py:245
  383.1 3.7 reshape.896
  389.4 5.1 fusion.118
  401.1 2.4 multiply_reduce_fusion.2
  404.8 2.2 multiply_convert_fusion.2
  407.1 3.8 fusion.39
  411.0 3.0 fusion.45
  415.2 3.7 copy.105
  419.0 5.2 multiply_reduce_fusion.1
  424.2 5.9 multiply_convert_fusion.1
  430.1 2.2 copy-done.3
  433.4 3.2 multiply_reduce_fusion
  436.7 4.6 multiply_convert_fusion
  441.3 4.4 fusion.48
  445.7 3.9 copy.104
  451.7 3.5 fusion.110
  456.7 2.0 fusion.109
  458.9 3.8 copy.103
  462.6 9.2 %pad_maximum_fusion = bf16[1,2048,3,192]{3,2,0,1:T(4,128)(2,1)S(1)} fusion(bf16[1,2048,1,192]{3,2,0,1:T(2,128)(2,1)S(1)} %copy-done.9, bf16[1,2048,1,192]{3,2,0,1:T(2,128)(2,1)} %copy.104, bf16[1,2048,1,192]{3,2,0,1:T(2,128)(2,1)} %copy.103), kind=kLoop, calls=%fused_computation.51 | loop fusion | flops 7077888 | bytes 4718592 | tf_op jit(solution)/shard_map/while/body/eval_jaxpr/stack | solution.py:130
  471.9 138.1 %all_to_all.55 = bf16[1,2048,3,192]{3,2,0,1:T(4,128)(2,1)} all-to-all(bf16[1,2048,3,192]{3,2,0,1:T(4,128)(2,1)S(1)} %pad_maximum_fusion), channel_id=1, replica_groups=mesh['fsdp'=8,'seq'=4] {'seq'}, dimensions={1} | all-to-all | bytes 4718592 | tf_op jit(solution)/shard_map/all_to_all | solution.py:252
  610.0 5.5 copy.106
  615.5 5.0 reshape.876
  620.4 4.1 copy.107
  628.5 5.2 fusion.114
  634.4 6.4 fusion.155
  640.8 5.4 fusion.156
  648.1 5.7 fusion.143
  655.3 2.0 convert_reduce_fusion.3
  657.3 42.2 %all-reduce.26 = (f32[2304]{0:T(1024)S(1)}, f32[768]{0:T(1024)S(1)}, f32[3072]{0:T(1024)S(1)}, f32[768]{0:T(1024)S(1)}, f32[768]{0:T(1024)S(1)}, /*index=5*/f32[768]{0:T(1024)S(1)}, f32[768]{0:T(1024)S(1)}) all-reduce(f32[2304]{0:T(1024)S(1)} %reduce_sum.254, ...), channel_id=3, replica_groups=mesh['fsdp'=8,'seq'=4] {'fsdp','seq'}, use_global_device_ids=true, to_apply=%region_20.21.clone | all-reduce | flops 9216 | bytes 73728
  703.1 43.7 %reduce-scatter.11.cloned.1.call-done = f32[96,768]{1,0:T(8,128)} async-done(((f32[3072,768]{1,0:T(8,128)}), f32[96,768]{1,0:T(8,128)}) %reduce-scatter.11.cloned.1.call-update) | async-done | bytes 294928 | tf_op jit(solution)/shard_map/reduce_scatter | solution.py:272
  746.8 125.6 %reduce-scatter.5.cloned.1.call-done = f32[24,2304]{1,0:T(8,128)} async-done(((f32[768,2304]{1,0:T(8,128)}), f32[24,2304]{1,0:T(8,128)}) %reduce-scatter.5.cloned.1.call-update) | async-done | bytes 221200 | tf_op jit(solution)/shard_map/reduce_scatter | solution.py:266
  (321 shorter events, 66.4 us)
Async XLA Ops:
  7.2 66.6 %all-gather.5.cloned.1.call-start = ((), (), s32[]{:S(2)}) async-start(), calls=%async_computation.8 | async-start | bytes 3649536 | tf_op jit(solution)/shard_map/all_gather | solution.py:154
  7.9 288.1 %all-gather.9.cloned.1.call-start = ((), (), s32[]{:S(2)}) async-start(), calls=%async_computation.10 | async-start | bytes 4866048 | tf_op jit(solution)/shard_map/all_gather | solution.py:158
  8.7 307.7 %all-gather.11.cloned.1.call-start = ((), (), s32[]{:S(2)}) async-start(), calls=%async_computation.11 | async-start | bytes 4866048 | tf_op jit(solution)/shard_map/all_gather | solution.py:160
  59.0 21.3 %copy-start.63 = (f32[768]{0:T(1024)}, f32[768]{0:T(1024)S(1)}, u32[]{:S(2)}) copy-start(f32[768]{0:T(1024)S(1)} %convert_element_type.187) | copy-start | bytes 9220
  59.0 21.3 %copy-start.78 = (f32[768]{0:T(1024)}, f32[768]{0:T(1024)S(1)}, u32[]{:S(2)}) copy-start(f32[768]{0:T(1024)S(1)} %convert_element_type.188) | copy-start | bytes 9220
  62.4 265.4 %copy-start.49 = (f32[512]{0:T(512)}, f32[512]{0:T(512)S(1)}, u32[]{:S(2)}) copy-start(f32[512]{0:T(512)S(1)} %fusion.135) | copy-start | bytes 6148
  62.6 27.7 %copy-start.51 = (f32[512,8]{0,1:T(8,128)}, f32[512,8]{0,1:T(8,128)S(1)}, u32[]{:S(2)}) copy-start(f32[512,8]{0,1:T(8,128)S(1)} %get-tuple-element.259) | copy-start | bytes 49156
  62.6 27.7 %copy-start.53 = (f32[512,8]{0,1:T(8,128)}, f32[512,8]{0,1:T(8,128)S(1)}, u32[]{:S(2)}) copy-start(f32[512,8]{0,1:T(8,128)S(1)} %get-tuple-element.260) | copy-start | bytes 49156
  94.5 94.0 %all-to-all-start = ((bf16[1,512,3,768]{1,2,0,3:T(4,128)(2,1)}), bf16[1,512,3,768]{1,2,0,3:T(4,128)(2,1)S(1)}, u32[]{:S(2)}, u32[]{:S(2)}) async-start(bf16[1,512,3,768]{1,2,0,3:T(4,128)(2,1)} %copy.92), calls=%async_computation | async-start | bytes 6291456 | tf_op jit(solution)/shard_map/all_to_all | solution.py:205
  98.2 236.9 %all-gather.7.cloned.1.call-start = ((), (), s32[]{:S(2)}) async-start(), calls=%async_computation.9 | async-start | bytes 1216512 | tf_op jit(solution)/shard_map/all_gather | solution.py:156
  197.2 5.4 copy-start.39
  198.2 7.9 copy-start.36
  198.2 27.2 %copy-start.34 = (bf16[512,1,192]{0,2,1:T(8,128)(2,1)}, bf16[512,1,192]{0,2,1:T(8,128)(2,1)S(1)}, u32[]{:S(2)}) copy-start(bf16[512,1,192]{0,2,1:T(8,128)(2,1)S(1)} %get-tuple-element.227) | copy-start | bytes 589828
  198.3 7.8 copy-start.10
  198.3 11.3 %copy-start.26 = (bf16[1536,1,192]{0,2,1:T(8,128)(2,1)}, bf16[1536,1,192]{0,2,1:T(8,128)(2,1)S(1)}, u32[]{:S(2)}) copy-start(bf16[1536,1,192]{0,2,1:T(8,128)(2,1)S(1)} %get-tuple-element.236) | copy-start | bytes 1769476
  198.5 16.6 %copy-start.18 = (bf16[2048,1,192]{0,2,1:T(8,128)(2,1)}, bf16[2048,1,192]{0,2,1:T(8,128)(2,1)S(1)}, u32[]{:S(2)}) copy-start(bf16[2048,1,192]{0,2,1:T(8,128)(2,1)S(1)} %get-tuple-element.237) | copy-start | bytes 2359300
  198.5 21.2 %copy-start.12 = (bf16[2048,1,192]{0,2,1:T(8,128)(2,1)}, bf16[2048,1,192]{0,2,1:T(8,128)(2,1)S(1)}, u32[]{:S(2)}) copy-start(bf16[2048,1,192]{0,2,1:T(8,128)(2,1)S(1)} %get-tuple-element.238) | copy-start | bytes 2359300
  202.6 3.5 copy-start.65
  208.2 3.5 copy-start.1
  208.2 3.5 copy-start.57
  209.6 5.5 copy-start.67
  211.7 3.4 copy-start.41
  211.7 3.4 copy-start.45
  217.8 4.6 copy-start
  217.8 4.6 copy-start.69
  219.7 5.8 copy-start.71
  235.1 21.8 %copy-start.83 = (bf16[768]{0:T(1024)(128)(2,1)S(1)}, bf16[768]{0:T(1024)(128)(2,1)}, u32[]{:S(2)}) copy-start(bf16[768]{0:T(1024)(128)(2,1)} %get-tuple-element.210) | copy-start | bytes 4612
  235.1 21.9 %copy-start.82 = (bf16[768]{0:T(1024)(128)(2,1)S(1)}, bf16[768]{0:T(1024)(128)(2,1)}, u32[]{:S(2)}) copy-start(bf16[768]{0:T(1024)(128)(2,1)} %get-tuple-element.211) | copy-start | bytes 4612
  235.1 21.9 %copy-start.77 = (bf16[3072]{0:T(1024)(128)(2,1)S(1)}, bf16[3072]{0:T(1024)(128)(2,1)}, u32[]{:S(2)}) copy-start(bf16[3072]{0:T(1024)(128)(2,1)} %get-tuple-element.212) | copy-start | bytes 18436
  252.7 24.7 %all-to-all-start.1 = ((bf16[4,2,49152]{2,1,0:T(2,128)(2,1)}), bf16[4,2,49152]{2,1,0:T(2,128)(2,1)}, u32[]{:S(2)}, u32[]{:S(2)}) async-start(bf16[4,2,49152]{2,1,0:T(2,128)(2,1)} %reshape.893), calls=%async_computation.1 | async-start | bytes 1572864 | tf_op jit(solution)/shard_map/all_to_all | solution.py:214
  256.9 446.2 %reduce-scatter.7.cloned.1.call-start = ((), (), s32[]{:S(2)}) async-start(), calls=%async_computation.13 | async-start | bytes 2433024 | tf_op jit(solution)/shard_map/reduce_scatter | solution.py:268
  295.9 407.1 %reduce-scatter.9.cloned.1.call-start = ((), (), s32[]{:S(2)}) async-start(), calls=%async_computation.14 | async-start | bytes 9732096 | tf_op jit(solution)/shard_map/reduce_scatter | solution.py:270
  316.4 13.1 %copy-start.6 = (bf16[1,512,768]{2,1,0:T(8,128)(2,1)S(1)}, bf16[1,512,768]{2,1,0:T(8,128)(2,1)}, u32[]{:S(2)}) copy-start(bf16[1,512,768]{2,1,0:T(8,128)(2,1)} %param.34) | copy-start | bytes 2359300
  335.0 411.8 %reduce-scatter.11.cloned.1.call-start = ((), (), s32[]{:S(2)}) async-start(), calls=%async_computation.15 | async-start | bytes 9732096 | tf_op jit(solution)/shard_map/reduce_scatter | solution.py:272
  394.6 477.8 %reduce-scatter.5.cloned.1.call-start = ((), (), s32[]{:S(2)}) async-start(), calls=%async_computation.12 | async-start | bytes 7299072 | tf_op jit(solution)/shard_map/reduce_scatter | solution.py:266
  397.5 6.0 copy-start.56
  398.2 8.9 %slice-start.6 = ((s8[9437184]{0:T(1024)(128)(4,1)}), s8[4194304]{0:T(1024)(128)(4,1)S(1)}, s32[]{:S(2)}) async-start(s8[9437184]{0:T(1024)(128)(4,1)} %bitcast.269), calls=%async_computation.22 | async-start | bytes 8388608
  399.1 4.4 copy-start.8
  401.1 5.9 slice-start.7
  403.5 3.5 slice-start.8
  404.8 6.2 slice-start
  404.8 6.2 slice-start.1
  407.0 7.0 copy-start.5
  407.1 3.9 slice-start.2
  407.1 3.9 copy-start.29
  414.1 4.9 copy-start.27
  414.1 4.9 copy-start.33
  418.9 14.3 %slice-start.3 = ((s8[12582912]{0:T(1024)(128)(4,1)}), s8[4194304]{0:T(1024)(128)(4,1)S(1)}, s32[]{:S(2)}) async-start(s8[12582912]{0:T(1024)(128)(4,1)} %bitcast.267), calls=%async_computation.19 | async-start | bytes 8388608
  418.9 14.3 %slice-start.4 = ((s8[12582912]{0:T(1024)(128)(4,1)}), s8[4194304]{0:T(1024)(128)(4,1)S(1)}, s32[]{:S(2)}) async-start(s8[12582912]{0:T(1024)(128)(4,1)} %bitcast.267), calls=%async_computation.20 | async-start | bytes 8388608
  424.2 8.1 copy-start.37
  424.2 9.1 %slice-start.5 = ((s8[12582912]{0:T(1024)(128)(4,1)}), s8[4194304]{0:T(1024)(128)(4,1)S(1)}, s32[]{:S(2)}) async-start(s8[12582912]{0:T(1024)(128)(4,1)} %bitcast.267), calls=%async_computation.21 | async-start | bytes 8388608
  436.7 4.6 copy-start.46
  441.3 8.3 copy-start.35
  445.7 6.0 copy-start.15
  445.7 11.0 %slice-start.11 = ((s8[6291456]{0:T(1024)(128)(4,1)}), s8[2097152]{0:T(1024)(128)(4,1)S(1)}, s32[]{:S(2)}) async-start(s8[6291456]{0:T(1024)(128)(4,1)} %bitcast.273), calls=%async_computation.27 | async-start | bytes 4194304
  449.6 5.5 copy-start.4
  449.6 5.5 copy-start.11
  451.7 5.1 slice-start.12
  458.8 3.9 copy-start.9
  634.3 6.4 copy-start.21
  640.7 5.4 copy-start.23
  640.8 5.4 copy-start.84
  648.1 5.7 copy-start.75
  699.6 173.3 %copy-start.85 = (f32[24]{0:T(128)}, f32[24]{0:T(128)S(1)}, u32[]{:S(2)}) copy-start(f32[24]{0:T(128)S(1)} %dynamic-slice.79) | copy-start | bytes 292
  (46 other events, 74.2 us)
Sparse Core Ops, SparseCore 0:
  10.8 62.9 all-gather.4
  76.6 98.6 all-gather.8
  178.0 66.2 all-gather.10
  247.0 59.7 all-gather.6
  312.5 101.8 reduce-scatter.6
  421.7 182.4 reduce-scatter.8
  610.7 136.1 reduce-scatter.10
  754.0 118.3 reduce-scatter.4
where the time goes:
time: 889 us; the launch traced here: 880 us
  waiting for transfers between devices  288 us (32%)
  blocking collectives  253 us (28%)
  matrix products  132 us (15%)
  local copies, waits for them, and re-layouts  118 us (13%)
  other arithmetic  64.2 us (7%)
  between operations  15.9 us (2%)
    all_to_all x1, blocking collectives, body(): lax.all_to_all(grad_turned_heads, 'seq', split_axis=1, concat_axis=3, til...  138 us
    reduce_scatter x1, waiting for transfers between devices, body(): lax.psum_scatter(grad_wqkv, ('fsdp', 'seq'), scatter_dimension=0, tiled=T...  126 us
    unnamed x2, blocking collectives  85.1 us
    all_to_all x1, waiting for transfers between devices, body(): lax.all_to_all(turned_low, 'seq', split_axis=3, concat_axis=1, tiled=True)  84.8 us
    unnamed x230, local copies, waits for them, and re-layouts  45 us
    reduce_scatter x1, waiting for transfers between devices, body(): lax.psum_scatter(grad_wdown, ('fsdp', 'seq'), scatter_dimension=0, tiled=...  43.7 us
    all_to_all x1, blocking collectives, body(): lax.all_to_all(grad_mixed, 'seq', split_axis=2, concat_axis=1, tiled=True)  30.2 us
    unnamed x7, other arithmetic  21 us
  transfers between devices with their start and end apart: 10, of which 5 were waited for; matrix products, arithmetic and copies ran while one was open for 33% of the time, Pallas kernels for 0%

commit v1 on v0

v1 whole, which is shorter than its diff:
```python
import math

import jax
import jax.numpy as jnp
from jax import lax
from jax.experimental import pallas as pl
from jax.experimental.pallas import tpu as pltpu
from jax.sharding import PartitionSpec as P

HEAD = 64
ROT = 16
mask_fill = -1e30
eps = 1e-05
BLK = 256
F32 = jnp.float32
BF = jnp.bfloat16


def rot_tables(positions):
    lane = lax.broadcasted_iota(jnp.int32, (1, 128), 1) % HEAD
    half = ROT // 2
    inv = jnp.exp((lane % half).astype(F32) * (-2.0 * math.log(10000.0) / ROT))
    ang = positions.astype(F32)[:, None] * inv
    cos, sin = jnp.cos(ang), jnp.sin(ang)
    c = jnp.where(lane < ROT, cos, 1.0)
    sa = jnp.where(lane < half, -sin, 0.0)
    sb = jnp.where((lane >= half) & (lane < ROT), sin, 0.0)
    return c, sa, sb

def nt(a, b):
    return lax.dot_general(a, b, (((1,), (1,)), ((), ())), preferred_element_type=F32)

def nn(a, b):
    return lax.dot_general(a, b, (((1,), (0,)), ((), ())), preferred_element_type=F32)

def attend(rank, proj, grad_mixed, tables):
    n, c, width = grad_mixed.shape
    heads = width // HEAD
    length = n * c
    half = ROT // 2
    nq = length // BLK
    scale = HEAD ** (-0.5)

    def kernel(rank_ref, proj_ref, gm_ref, c_ref, sa_ref, sb_ref, mixed_ref, gp_ref, sum_ref,
               q_s, k_s, v_s, d_s, dk_s, dv_s, s_s, dp_s, p_s):
        rank = rank_ref[0]

        def spin(x, at, sign):
            cc, sa, sb = c_ref[at], sa_ref[at], sb_ref[at]
            left = pltpu.roll(x, 128 - half, 1)
            right = pltpu.roll(x, half, 1)
            return x * cc + sign * (left * sa + right * sb)

        def load(chunk, carry):
            at = lax.rem(rank - chunk + n, n)
            rows = pl.ds(pl.multiple_of(chunk * c, c), c)
            for tile in range(2 * width // 128):
                x = spin(proj_ref[at, :, tile * 128:(tile + 1) * 128], at, 1.0)
                for side in range(2):
                    slot = tile * 2 + side
                    piece = x[:, side * HEAD:(side + 1) * HEAD].astype(BF)
                    if slot < heads:
                        q_s[slot, rows, :] = piece * jnp.asarray(scale, BF)
                    else:
                        k_s[slot - heads, rows, :] = piece
            for h in range(heads):
                v_s[h, rows, :] = proj_ref[at, :, 2 * width + h * HEAD:2 * width + (h + 1) * HEAD].astype(BF)
                d_s[h, rows, :] = gm_ref[at, :, h * HEAD:(h + 1) * HEAD]
            return carry
        lax.fori_loop(0, n, load, 0)

        def one_head(h, carry):
            dk_s[h] = jnp.zeros((length, HEAD), F32)
            dv_s[h] = jnp.zeros((length, HEAD), F32)
            row = lax.broadcasted_iota(jnp.int32, (BLK, BLK), 0)
            col = lax.broadcasted_iota(jnp.int32, (BLK, BLK), 1)
            tri = row <= col
            for i in range(nq):
                span = slice(i * BLK, (i + 1) * BLK)
                qi = q_s[h, span, :]
                di = d_s[h, span, :]
                top = jnp.full((8, BLK), mask_fill, F32)
                for j in range(i + 1):
                    s = nt(k_s[h, j * BLK:(j + 1) * BLK, :], qi)
                    if j == i:
                        s = jnp.where(tri, s, mask_fill)
                    s_s[j] = s
                    top = jnp.maximum(top, jnp.max(s.reshape(BLK // 8, 8, BLK), axis=0))
                top = jnp.max(top, axis=0, keepdims=True)
                tot = jnp.zeros((8, BLK), F32)
                for j in range(i + 1):
                    e = jnp.exp(s_s[j] - top)
                    s_s[j] = e
                    tot = tot + jnp.sum(e.reshape(BLK // 8, 8, BLK), axis=0)
                inv = 1.0 / jnp.sum(tot, axis=0, keepdims=True)
                out = jnp.zeros((HEAD, BLK), F32)
                delta = jnp.zeros((8, BLK), F32)
                for j in range(i + 1):
                    keys = slice(j * BLK, (j + 1) * BLK)
                    p = s_s[j] * inv
                    s_s[j] = p
                    low = p.astype(BF)
                    dp = nt(v_s[h, keys, :], di)
                    dp_s[j] = dp
                    delta = delta + jnp.sum((p * dp).reshape(BLK // 8, 8, BLK), axis=0)
                    out = out + nn(v_s[h, keys, :].T, low)
                    dv_s[h, keys, :] = dv_s[h, keys, :] + nn(low, di)
                delta = jnp.sum(delta, axis=0, keepdims=True)
                dq = jnp.zeros((HEAD, BLK), F32)
                for j in range(i + 1):
                    keys = slice(j * BLK, (j + 1) * BLK)
                    ds = (s_s[j] * (dp_s[j] - delta)).astype(BF)
                    dq = dq + nn(k_s[h, keys, :].T, ds)
                    dk_s[h, keys, :] = dk_s[h, keys, :] + nn(ds, qi)
                q_s[h, span, :] = (dq * scale).T.astype(BF)
                d_s[h, span, :] = out.T.astype(BF)
            return carry
        lax.fori_loop(0, heads, one_head, 0)

        sum_ref[...] = jnp.zeros_like(sum_ref)

        def store(chunk, carry):
            at = lax.rem(rank - chunk + n, n)
            rows = pl.ds(pl.multiple_of(chunk * c, c), c)
            for tile in range(2 * width // 128):
                pieces = []
                for side in range(2):
                    slot = tile * 2 + side
                    if slot < heads:
                        pieces.append(q_s[slot, rows, :].astype(F32))
                    else:
                        pieces.append(dk_s[slot - heads, rows, :].astype(BF).astype(F32))
                x = spin(jnp.concatenate(pieces, axis=1), at, -1.0).astype(BF)
                lanes = slice(tile * 128, (tile + 1) * 128)
                gp_ref[at, :, lanes] = x
                sum_ref[:, lanes] += jnp.sum(x.astype(F32).reshape(c // 8, 8, 128), axis=0)
            x = jnp.concatenate([dv_s[h, rows, :].astype(BF) for h in range(heads)], axis=1)
            gp_ref[at, :, 2 * width:] = x
            sum_ref[:, 2 * width:] += jnp.sum(x.astype(F32).reshape(c // 8, 8, width), axis=0)
            mixed_ref[at] = jnp.concatenate([d_s[h, rows, :] for h in range(heads)], axis=1)
            return carry
        lax.fori_loop(0, n, store, 0)

    vm = pl.BlockSpec(memory_space=pltpu.VMEM)
    flops = 6 * heads * length * length * HEAD
    return pl.pallas_call(
        kernel,
        out_shape=(
            jax.ShapeDtypeStruct((n, c, width), BF),
            jax.ShapeDtypeStruct((n, c, 3 * width), BF),
            jax.ShapeDtypeStruct((8, 3 * width), F32),
        ),
        in_specs=[pl.BlockSpec(memory_space=pltpu.SMEM)] + [vm] * 5,
        out_specs=(vm, vm, vm),
        scratch_shapes=[pltpu.VMEM((heads, length, HEAD), BF)] * 4
        + [pltpu.VMEM((heads, length, HEAD), F32)] * 2
        + [pltpu.VMEM((nq, BLK, BLK), F32)] * 2 + [pltpu.VMEM((8, 128), BF)],
        compiler_params=pltpu.CompilerParams(vmem_limit_bytes=56 << 20),
        cost_estimate=pl.CostEstimate(flops=flops * 4, bytes_accessed=16 << 20, transcendentals=heads * length * length // 2),
        name="attend",
    )(rank, proj, grad_mixed, *tables)


def tn(a, b):
    return lax.dot_general(a, b, (((0,), (0,)), ((), ())), preferred_element_type=F32)


def make_body(nf, n):
    both = ("fsdp", "seq")

    def send(x, k):
        return lax.ppermute(x, "seq", [(i, (i + k) % n) for i in range(n)])

    def body(
        tokens,
        cotangent,
        w_qkv,
        b_qkv,
        w_out,
        b_out,
        w_up,
        b_up,
        w_down,
        b_down,
        gain_attn,
        shift_attn,
        gain_mlp,
        shift_mlp,
    ):
        rank = lax.axis_index("seq")
        _, c, d = tokens.shape
        rows = w_qkv.shape[0]
        width = d // n
        units = w_down.shape[0]
        tok = tokens.reshape(c, d)
        cot = cotangent.reshape(c, d)

        toks = [tok] + [send(tok, k) for k in range(1, n)]

        full_out = lax.all_gather(w_out, both, axis=0, tiled=True)
        qkv_cols = w_qkv.reshape(rows, 3, n, width).transpose(2, 0, 1, 3).reshape(n, rows, 3 * width)
        up_cols = w_up.reshape(rows, nf, n, units).transpose(2, 0, 1, 3).reshape(n, rows, nf * units)
        cols = jnp.concatenate([qkv_cols, up_cols], axis=2)
        cols = lax.all_to_all(cols, "seq", split_axis=0, concat_axis=0, tiled=True)
        cols = lax.all_gather(cols.reshape(n * rows, -1), "fsdp", axis=0, tiled=True)
        own_qkv = cols[:, : 3 * width]
        own_up = cols[:, 3 * width :]
        own_down = lax.all_gather(w_down, "fsdp", axis=0, tiled=True)

        vectors = (b_qkv, b_out, b_up, b_down, gain_attn, shift_attn, gain_mlp, shift_mlp)
        lengths = [v.shape[0] for v in vectors]
        pad = -sum(lengths) % 1024
        pack = jnp.concatenate(vectors + (jnp.zeros((pad,), BF),)).reshape(-1, 128)
        packs = lax.all_gather(pack, both, axis=0, tiled=True).reshape(nf * n, -1)
        full = []
        at = 0
        for size in lengths:
            full.append(packs[:, at : at + size].reshape(-1).astype(F32))
            at += size
        bias_qkv, bias_out, bias_up, bias_down, gain_one, shift_one, gain_two, shift_two = full
        own_bias_qkv = lax.dynamic_index_in_dim(
            bias_qkv.reshape(3, n, width), rank, 1, keepdims=False
        ).reshape(-1)
        own_bias_up = lax.dynamic_index_in_dim(
            bias_up.reshape(nf, n, units), rank, 1, keepdims=False
        ).reshape(-1)

        out_blocks = [
            lax.dynamic_slice_in_dim(full_out, (rank + k) % n * width, width, 0) for k in range(n)
        ]
        grad_mixed = []
        for k in range(n):
            part = nt(cot, out_blocks[k]).astype(BF)
            grad_mixed.append(send(part, k) if k else part)

        late_cot, toks[-1] = lax.optimization_barrier((cot, toks[-1]))
        cots = [cot] + [send(late_cot, k) for k in range(1, n)]

        hats, ones, twos, scales, projected = [], [], [], [], []
        for k in range(n):
            x = toks[k].astype(F32)
            centred = x - jnp.mean(x, axis=-1, keepdims=True)
            spread = lax.rsqrt(jnp.mean(centred * centred, axis=-1, keepdims=True) + eps)
            hat = centred * spread
            hats.append(hat)
            scales.append(spread)
            ones.append((hat * gain_one + shift_one).astype(BF))
            twos.append((hat * gain_two + shift_two).astype(BF))
            projected.append(nn(ones[k], own_qkv) + own_bias_qkv)
        tables = [
            [t for t in rot_tables(((rank - k) % n) * c + jnp.arange(c, dtype=jnp.int32))]
            for k in range(n)
        ]
        tables = [jnp.stack(t) for t in zip(*tables)]

        pres, hiddens = [], []
        mlp_out = None
        for k in range(n):
            pre = nn(twos[k], own_up) + own_bias_up
            hidden = jax.nn.gelu(pre, approximate=False).astype(BF)
            pres.append(pre)
            hiddens.append(hidden)
            part = nn(hidden, own_down)
            part = send(part.astype(BF), -k).astype(F32) if k else part
            mlp_out = part if mlp_out is None else mlp_out + part

        mixed, grad_proj, sum_qkv = attend(
            jnp.full((1,), rank, jnp.int32), jnp.stack(projected), jnp.stack(grad_mixed), tables
        )

        cot_float = cot.astype(F32)
        grad_pres, incoming = [], []
        sum_up = sum_gain_two = sum_shift_two = 0.0
        for k in range(n):
            grad_hidden = nt(cots[k], own_down)
            pre = pres[k]
            slope = 0.5 * (1.0 + lax.erf(pre * math.sqrt(0.5))) + pre * jnp.exp(
                -0.5 * pre * pre
            ) * (1.0 / math.sqrt(2.0 * math.pi))
            grad_pre = (grad_hidden * slope).astype(BF)
            grad_pres.append(grad_pre)
            sum_up += jnp.sum(grad_pre.astype(F32), axis=0)
            arriving = nt(grad_pre, own_up)
            sum_gain_two += jnp.sum(arriving * hats[k], axis=0)
            sum_shift_two += jnp.sum(arriving, axis=0)
            incoming.append(arriving * gain_two)
        hidden_all = jnp.concatenate(hiddens)
        cot_all = jnp.concatenate(cots)
        one_all = jnp.concatenate(ones)
        two_all = jnp.concatenate(twos)
        grad_down = tn(hidden_all, cot_all)
        grad_up = tn(two_all, jnp.concatenate(grad_pres))

        def reduce_rows(grad):
            return lax.psum_scatter(grad.astype(BF), "fsdp", scatter_dimension=0, tiled=True)

        def to_owners(grad):
            grad = reduce_rows(grad).reshape(n, rows, -1)
            return lax.all_to_all(grad, "seq", split_axis=0, concat_axis=0, tiled=True).astype(F32)

        grad_w_down = reduce_rows(grad_down).astype(F32)
        grad_w_up = (
            to_owners(grad_up).reshape(n, rows, nf, units).transpose(1, 2, 0, 3).reshape(rows, -1)
        )

        attn_out = None
        grad_out = jnp.zeros((n, width, d), F32)
        for k in range(n):
            part = send(mixed[k], -k) if k else mixed[k]
            term = nn(part, out_blocks[k])
            attn_out = term if attn_out is None else attn_out + term
            grad_out = lax.dynamic_update_index_in_dim(grad_out, tn(part, cot), (rank + k) % n, 0)
        block_out = tok.astype(F32) + attn_out + bias_out + mlp_out + bias_down
        grad_w_out = lax.psum_scatter(
            grad_out.reshape(d, d).astype(BF), both, scatter_dimension=0, tiled=True
        ).astype(F32)

        grad_q = None
        sum_gain_one = sum_shift_one = 0.0
        for k in range(n):
            arriving = nt(grad_proj[k], own_qkv)
            sum_gain_one += jnp.sum(arriving * hats[k], axis=0)
            sum_shift_one += jnp.sum(arriving, axis=0)
            part = arriving * gain_one + incoming[k]
            part = send(part.astype(BF), -k).astype(F32) if k else part
            grad_q = part if grad_q is None else grad_q + part
        grad_qkv = tn(one_all, grad_proj.reshape(n * c, -1))
        grad_w_qkv = (
            to_owners(grad_qkv).reshape(n, rows, 3, width).transpose(1, 2, 0, 3).reshape(rows, -1)
        )
        grad_tokens = cot_float + scales[0] * (
            grad_q
            - jnp.mean(grad_q, axis=-1, keepdims=True)
            - hats[0] * jnp.mean(grad_q * hats[0], axis=-1, keepdims=True)
        )

        def place(values, parts):
            blank = jnp.zeros((parts, n, values.size // parts), F32)
            filled = lax.dynamic_update_index_in_dim(blank, values.reshape(parts, -1), rank, 1)
            return filled.reshape(-1)

        sum_out = jnp.sum(cot_float, axis=0)
        sums = (
            place(jnp.sum(sum_qkv, axis=0), 3),
            sum_out,
            place(sum_up, nf),
            sum_out,
            sum_gain_one,
            sum_shift_one,
            sum_gain_two,
            sum_shift_two,
        )
        packed = jnp.concatenate(
            [s.reshape(nf * n, -1) for s in sums] + [jnp.zeros((nf * n, pad), F32)], axis=1
        )
        packed = lax.psum_scatter(
            packed.reshape(-1, 128), both, scatter_dimension=0, tiled=True
        ).reshape(-1)
        grads = []
        at = 0
        for size in lengths:
            grads.append(packed[at : at + size])
            at += size

        return (
            block_out.astype(BF).reshape(tokens.shape),
            grad_tokens.astype(BF).reshape(tokens.shape),
            grad_w_qkv,
            grads[0],
            grad_w_out,
            grads[1],
            grad_w_up,
            grads[2],
            grad_w_down,
            grads[3],
            grads[4],
            grads[5],
            grads[6],
            grads[7],
        )

    return body


def solution(mesh):
    tok = P("fsdp", "seq", None)
    mat = P(("fsdp", "seq"), None)
    vec = P(("fsdp", "seq"))
    params = (mat, vec, mat, vec, mat, vec, mat, vec, vec, vec, vec, vec)
    return jax.shard_map(
        make_body(mesh.shape["fsdp"], mesh.shape["seq"]),
        mesh=mesh,
        in_specs=(tok, tok) + params,
        out_specs=(tok, tok) + params,
        check_vma=False,
    )
```

time: 889 us -> 780 us (0.88)
  blocking collectives: 253 us -> 140 us
  local copies, waits for them, and re-layouts: 118 us -> 20.6 us
  waiting for transfers between devices: 288 us -> 368 us
  Pallas kernels: 0 us -> 44.2 us
  starting transfers between devices: 8.38 us -> 50.5 us
  other arithmetic: 64.2 us -> 28.9 us
  matrix products: 132 us -> 102 us
    all_to_all x2 -> x1, blocking collectives: 168 us -> 15.3 us  [body(): cols = lax.all_to_all(cols, 'seq', split_axis=0, concat_axis=0, tiled=True)]
    all_gather x0 -> x1, blocking collectives: none -> 125 us  [body(): packs = lax.all_gather(pack, both, axis=0, tiled=True).reshape(nf * n, -1)]
    ppermute x0 -> x18, waiting for transfers between devices: none -> 121 us  [send(): return lax.ppermute(x, 'seq', [(i, (i + k) % n) for i in range(n)])]
    all_to_all x2, waiting for transfers between devices: 105 us -> 0.01 us  [to_owners(): lax.all_to_all(grad, 'seq', split_axis=0, concat_axis=0, tiled=True)]
    unnamed x2 -> x0, blocking collectives: 85.1 us -> none
    unnamed x8 -> x9, waiting for transfers between devices: 2.47 us -> 77.8 us
    pallas_call x0 -> x1, Pallas kernels: none -> 44.2 us  [attend(): pl.pallas_call(kernel, out_shape=(jax.ShapeDtypeStruct((n, c, width), BF)...]
    ppermute x0 -> x18, starting transfers between devices: none -> 41.3 us  [send(): return lax.ppermute(x, 'seq', [(i, (i + k) % n) for i in range(n)])]
  transfers between devices with their start and end apart: 10 -> 28, of which waited for: 5 -> 11; matrix products, arithmetic and copies ran while one was open for 33% -> 19% of each run, Pallas kernels for 0% -> 6%
where the time goes in v1:
time: 780 us; the launch traced here: 771 us
  waiting for transfers between devices  368 us (47%)
  blocking collectives  140 us (18%)
  matrix products  102 us (13%)
  starting transfers between devices  50.5 us (6%)
  Pallas kernels  44.2 us (6%)
  other arithmetic  28.9 us (4%)
  local copies, waits for them, and re-layouts  20.6 us (3%)
  between operations  15.5 us (2%)
    all_gather x1, blocking collectives, body(): packs = lax.all_gather(pack, both, axis=0, tiled=True).reshape(nf * n, -1)  125 us
    ppermute x18, waiting for transfers between devices, send(): return lax.ppermute(x, 'seq', [(i, (i + k) % n) for i in range(n)])  121 us
    reduce_scatter x1, waiting for transfers between devices, body(): lax.psum_scatter(grad_out.reshape(d, d).astype(BF), both, scatter_dimensi...  94.8 us
    unnamed x9, waiting for transfers between devices  77.8 us
    reduce_scatter x3, waiting for transfers between devices, reduce_rows(): lax.psum_scatter(grad.astype(BF), 'fsdp', scatter_dimension=0, tiled=True)  75.2 us
    dot_general x16, matrix products, nn(): lax.dot_general(a, b, (((1,), (0,)), ((), ())), preferred_element_type=F32)  56.3 us
    pallas_call x1, Pallas kernels, attend(): pl.pallas_call(kernel, out_shape=(jax.ShapeDtypeStruct((n, c, width), BF)...  44.2 us
    ppermute x18, starting transfers between devices, send(): return lax.ppermute(x, 'seq', [(i, (i + k) % n) for i in range(n)])  41.3 us
  transfers between devices with their start and end apart: 28, of which 11 were waited for; matrix products, arithmetic and copies ran while one was open for 19% of the time, Pallas kernels for 6%

profile of v1, /device:TPU:0, one launch (start us, length us, event | category | flops | bytes accessed | tf_op | source)
XLA Modules:
  0.0 770.8 jit_solution(4141485793173788513)
XLA Ops:
  8.0 1.1 reshape.1186
  10.9 15.3 %all_to_all.15 = bf16[4,24,1344]{2,1,0:T(8,128)(2,1)} all-to-all(bf16[4,24,1344]{2,1,0:T(8,128)(2,1)S(1)} %pad_maximum_fusion.5), channel_id=1, replica_groups=mesh['fsdp'=8,'seq'=4] {'seq'}, dimensions={0} | all-to-all | bytes 516096 | tf_op jit(solution)/shard_map/all_to_all | solution.py:204
  26.3 1.6 collective-permute-start.2
  29.5 124.9 %all_gather.12 = bf16[256,128]{1,0:T(8,128)(2,1)S(1)} all-gather(bf16[8,128]{1,0:T(8,128)(2,1)S(1)} %bitcast.179), channel_id=1, replica_groups=mesh['fsdp'=8,'seq'=4] {'fsdp','seq'}, dimensions={0}, use_global_device_ids=true | all-gather | bytes 67584 | tf_op jit(solution)/shard_map/all_gather | solution.py:214
  154.6 3.8 fusion.205
  162.8 1.1 collective-permute-start.12
  165.1 1.3 convert_reduce_fusion.4
  166.4 1.5 fusion.94
  167.9 4.6 fusion.75
  172.5 1.4 convolution_convert_fusion.5
  174.7 2.3 collective-permute-start.3
  177.1 1.4 convolution_convert_fusion.4
  180.3 1.4 convolution_convert_fusion.3
  182.5 2.5 collective-permute-start.5
  185.0 2.0 convolution_convert_fusion.6
  188.1 18.1 %collective-permute-done.3 = bf16[512,192]{1,0:T(8,128)(2,1)} collective-permute-done((bf16[512,192]{1,0:T(8,128)(2,1)}, bf16[512,192]{1,0:T(8,128)(2,1)}, u32[]{:S(2)}, u32[]{:S(2)}) %collective-permute-start.3) | collective-permute-done | bytes 196640 | tf_op jit(solution)/shard_map/ppermute | solution.py:172
  206.5 22.2 %collective-permute-done.4 = bf16[512,192]{1,0:T(8,128)(2,1)} collective-permute-done((bf16[512,192]{1,0:T(8,128)(2,1)}, bf16[512,192]{1,0:T(8,128)(2,1)}, u32[]{:S(2)}, u32[]{:S(2)}) %collective-permute-start.4) | collective-permute-done | bytes 196640 | tf_op jit(solution)/shard_map/ppermute | solution.py:172
  228.7 2.3 pad_maximum_fusion.1.gm_ref
  231.0 2.4 fusion.177
  236.5 2.7 pad_maximum_fusion.proj_ref
  239.1 44.2 %attend.1 = (bf16[4,512,192]{2,1,0:T(8,128)(2,1)}, bf16[4,512,576]{2,1,0:T(8,128)(2,1)}, f32[8,576]{1,0:T(8,128)}) custom-call(s32[1]{0:T(128)} %bitcast.1.rank_ref, f32[4,512,576]{2,1,0:T(8,128)} %pad_maximum_fusion.proj_ref, bf16[4,512,192]{2,1,0:T(8,128)(2,1)} %pad_maximum_fusion.1.gm_ref, f32[4,512,128]{2,1,0:T(8,128)} %pad_maximum_fusion.2.c_ref, ...), custom_call_target="tpu_custom_call" | custom-call | flops 19327352832 | bytes 16777216 | tf_op jit(solution)/shard_map/attend/pallas_call | solution.py:146
  283.4 15.5 %fusion.105 = (bf16[512,768]{1,0:T(8,128)(2,1)}, f32[512,768]{1,0:T(8,128)}) fusion(f32[768]{0:T(1024)S(1)} %add.583, bf16[512,768]{1,0:T(8,128)(2,1)S(1)} %copy-done.11, bf16[768,1344]{1,0:T(8,128)(2,1)S(1)} %copy-done.21), kind=kOutput, calls=%fused_computation.125 | convolution fusion | flops 629932032 | bytes 4329472 | tf_op jit(solution)/shard_map/dot_general | solution.py:34
  298.9 3.2 convert_reduce_fusion.7
  304.2 3.3 fusion.278
  307.5 22.7 %collective-permute-start.13 = (bf16[512,768]{1,0:T(8,128)(2,1)}, bf16[512,768]{1,0:T(8,128)(2,1)}, u32[]{:S(2)}, u32[]{:S(2)}) collective-permute-start(bf16[512,768]{1,0:T(8,128)(2,1)} %get-tuple-element.48), channel_id=1, source_target_pairs={{0,3},{1,0},{2,1},{3,2},{4,7},{5,4},{6,5},{7,6},{8,11},{9,8},{10,9... | collective-permute-start | bytes 2359304 | tf_op jit(solution)/shard_map/ppermute | solution.py:172
  330.1 5.1 fusion.108
  335.3 2.2 convert_reduce_fusion.6
  339.4 2.1 fusion.280
  341.4 5.2 fusion.111
  346.6 2.2 convert_reduce_fusion.5
  350.7 2.1 fusion.281
  353.7 3.6 fusion.174
  357.3 6.5 fusion.102
  363.9 1.1 convert_reduce_fusion.8
  365.5 2.4 fusion.193
  368.8 26.8 %collective-permute-done.15 = bf16[512,768]{1,0:T(8,128)(2,1)S(1)} collective-permute-done((bf16[512,768]{1,0:T(8,128)(2,1)}, bf16[512,768]{1,0:T(8,128)(2,1)S(1)}, u32[]{:S(2)}, u32[]{:S(2)}) %collective-permute-start.15) | collective-permute-done | bytes 786464 | tf_op jit(solution)/shard_map/ppermute | solution.py:172
  396.4 3.0 fusion.279
  399.8 1.6 convert_reduce_fusion.1
  402.6 6.5 fusion.169
  410.4 3.6 collective-permute-start.7
  414.0 1.9 collective-permute-start.8
  416.0 1.3 fusion.184
  417.4 1.3 collective-permute-done.6
  419.0 18.7 %collective-permute-done.7 = bf16[512,192]{1,0:T(8,128)(2,1)S(1)} collective-permute-done((bf16[512,192]{1,0:T(8,128)(2,1)S(1)}, bf16[512,192]{1,0:T(8,128)(2,1)S(1)}, u32[]{:S(2)}, u32[]{:S(2)}) %collective-permute-start.7) | collective-permute-done | bytes 196640 | tf_op jit(solution)/shard_map/ppermute | solution.py:172
  439.6 3.3 convolution_convert_fusion.1
  442.9 1.7 convolution_convert_fusion.2
  444.6 1.7 convolution_convert_fusion
  446.3 2.0 collective-permute-start.11
  448.3 5.3 fusion.164
  453.7 3.2 fusion.288
  456.9 1.4 fusion.216
  458.3 1.5 fusion.226
  459.9 1.6 fusion.223
  461.4 4.2 all-to-all-start.1
  465.6 11.0 %collective-permute-done.10 = bf16[512,768]{1,0:T(8,128)(2,1)} collective-permute-done((bf16[512,768]{1,0:T(8,128)(2,1)}, bf16[512,768]{1,0:T(8,128)(2,1)}, u32[]{:S(2)}, u32[]{:S(2)}) %collective-permute-start.10) | collective-permute-done | bytes 786464 | tf_op jit(solution)/shard_map/ppermute | solution.py:172
  476.6 22.3 %collective-permute-done.9 = bf16[512,768]{1,0:T(8,128)(2,1)} collective-permute-done((bf16[512,768]{1,0:T(8,128)(2,1)}, bf16[512,768]{1,0:T(8,128)(2,1)}, u32[]{:S(2)}, u32[]{:S(2)}) %collective-permute-start.9) | collective-permute-done | bytes 786464 | tf_op jit(solution)/shard_map/ppermute | solution.py:172
  498.9 4.9 fusion.186
  503.8 77.0 %all-reduce.3.cloned.1.call-done = f32[256,128]{1,0:T(8,128)} async-done(((f32[256,128]{1,0:T(8,128)}), f32[256,128]{1,0:T(8,128)}) %all-reduce.3.cloned.1.call-update) | async-done | bytes 131088
  582.6 37.5 %reduce-scatter.9.cloned.1.call-done = bf16[96,768]{1,0:T(8,128)(2,1)} async-done(((bf16[768,768]{1,0:T(8,128)(2,1)}), bf16[96,768]{1,0:T(8,128)(2,1)}) %reduce-scatter.9.cloned.1.call-update) | async-done | bytes 147472 | tf_op jit(solution)/shard_map/reduce_scatter | solution.py:295
  620.1 4.6 all-to-all-start.2
  626.6 94.8 %reduce-scatter.7.cloned.1.call-done = bf16[24,768]{1,0:T(8,128)(2,1)} async-done(((bf16[768,768]{1,0:T(8,128)(2,1)}), bf16[24,768]{1,0:T(8,128)(2,1)}) %reduce-scatter.7.cloned.1.call-update) | async-done | bytes 36880 | tf_op jit(solution)/shard_map/reduce_scatter | solution.py:314
  721.4 1.4 convert_element_type.355
  722.8 37.7 %reduce-scatter.11.cloned.1.call-done = bf16[96,768]{1,0:T(8,128)(2,1)} async-done(((bf16[768,768]{1,0:T(8,128)(2,1)}), bf16[96,768]{1,0:T(8,128)(2,1)}) %reduce-scatter.11.cloned.1.call-update) | async-done | bytes 147472 | tf_op jit(solution)/shard_map/reduce_scatter | solution.py:295
  760.6 1.6 convert_element_type.358
  (227 shorter events, 36.3 us)
Async XLA Ops:
  7.2 165.3 %all-gather.6.cloned.1.call-start = ((), (), s32[]{:S(2)}) async-start(), calls=%async_computation.8 | async-start | bytes 1216512 | tf_op jit(solution)/shard_map/all_gather | solution.py:200
  7.9 223.1 %all-gather.4.cloned.1.call-start = ((), (), s32[]{:S(2)}) async-start(), calls=%async_computation.7 | async-start | bytes 2433024 | tf_op jit(solution)/shard_map/all_gather | solution.py:205
  9.1 17.2 %copy-start.1 = (bf16[1,512,768]{2,1,0:T(8,128)(2,1)S(1)}, bf16[1,512,768]{2,1,0:T(8,128)(2,1)}, u32[]{:S(2)}) copy-start(bf16[1,512,768]{2,1,0:T(8,128)(2,1)} %param.14) | copy-start | bytes 2359300
  10.4 18.9 %copy-start.26 = (bf16[72]{0:T(256)(128)(2,1)S(1)}, bf16[72]{0:T(256)(128)(2,1)}, u32[]{:S(2)}) copy-start(bf16[72]{0:T(256)(128)(2,1)} %param.17) | copy-start | bytes 436
  10.4 18.9 %copy-start.27 = (bf16[24]{0:T(256)(128)(2,1)S(1)}, bf16[24]{0:T(256)(128)(2,1)}, u32[]{:S(2)}) copy-start(bf16[24]{0:T(256)(128)(2,1)} %param.19) | copy-start | bytes 148
  10.4 18.9 %copy-start.28 = (bf16[96]{0:T(256)(128)(2,1)S(1)}, bf16[96]{0:T(256)(128)(2,1)}, u32[]{:S(2)}) copy-start(bf16[96]{0:T(256)(128)(2,1)} %param.21) | copy-start | bytes 580
  10.4 18.9 %copy-start.29 = (bf16[24]{0:T(256)(128)(2,1)S(1)}, bf16[24]{0:T(256)(128)(2,1)}, u32[]{:S(2)}) copy-start(bf16[24]{0:T(256)(128)(2,1)} %param.23) | copy-start | bytes 148
  10.5 18.9 %copy-start.30 = (bf16[24]{0:T(256)(128)(2,1)S(1)}, bf16[24]{0:T(256)(128)(2,1)}, u32[]{:S(2)}) copy-start(bf16[24]{0:T(256)(128)(2,1)} %param.24) | copy-start | bytes 148
  10.5 18.9 %copy-start.31 = (bf16[24]{0:T(256)(128)(2,1)S(1)}, bf16[24]{0:T(256)(128)(2,1)}, u32[]{:S(2)}) copy-start(bf16[24]{0:T(256)(128)(2,1)} %param.25) | copy-start | bytes 148
  10.5 18.9 %copy-start.32 = (bf16[24]{0:T(256)(128)(2,1)S(1)}, bf16[24]{0:T(256)(128)(2,1)}, u32[]{:S(2)}) copy-start(bf16[24]{0:T(256)(128)(2,1)} %param.26) | copy-start | bytes 148
  10.5 18.9 %copy-start.33 = (bf16[24]{0:T(256)(128)(2,1)S(1)}, bf16[24]{0:T(256)(128)(2,1)}, u32[]{:S(2)}) copy-start(bf16[24]{0:T(256)(128)(2,1)} %param.27) | copy-start | bytes 148
  26.2 272.7 %all-gather.8.cloned.1.call-start = ((), (), s32[]{:S(2)}) async-start(), calls=%async_computation.9 | async-start | bytes 1327104 | tf_op jit(solution)/shard_map/all_gather | solution.py:208
  26.3 136.4 %collective-permute-start.2 = (bf16[512,768]{1,0:T(8,128)(2,1)S(1)}, bf16[512,768]{1,0:T(8,128)(2,1)S(1)}, u32[]{:S(2)}, u32[]{:S(2)}) collective-permute-start(bf16[512,768]{1,0:T(8,128)(2,1)S(1)} %bitcast.161), channel_id=1, source_target_pairs={{0,3},{1,0},{2,1},{3,2},{4,7},{5,4},{6,5},{7,6},{8,11},{9,8},{10,9... | collective-permute-start | bytes 2359304 | tf_op jit(solution)/shard_map/ppermute | solution.py:172
  27.9 136.2 %collective-permute-start.1 = (bf16[512,768]{1,0:T(8,128)(2,1)S(1)}, bf16[512,768]{1,0:T(8,128)(2,1)S(1)}, u32[]{:S(2)}, u32[]{:S(2)}) collective-permute-start(bf16[512,768]{1,0:T(8,128)(2,1)S(1)} %bitcast.162), channel_id=1, source_target_pairs={{0,2},{1,3},{2,0},{3,1},{4,6},{5,7},{6,4},{7,5},{8,10},{9,11},{10,... | collective-permute-start | bytes 2359304 | tf_op jit(solution)/shard_map/ppermute | solution.py:172
  28.3 136.7 %collective-permute-start = (bf16[512,768]{1,0:T(8,128)(2,1)S(1)}, bf16[512,768]{1,0:T(8,128)(2,1)}, u32[]{:S(2)}, u32[]{:S(2)}) collective-permute-start(bf16[512,768]{1,0:T(8,128)(2,1)S(1)} %bitcast.163), channel_id=1, source_target_pairs={{0,1},{1,2},{2,3},{3,0},{4,5},{5,6},{6,7},{7,4},{8,9},{9,10},{10,1... | collective-permute-start | bytes 2359304 | tf_op jit(solution)/shard_map/ppermute | solution.py:172
  29.0 432.4 %reduce-scatter.5.cloned.1.call-start = ((), (), s32[]{:S(2)}) async-start(), calls=%async_computation.10 | async-start | bytes 1105920 | tf_op jit(solution)/shard_map/reduce_scatter | solution.py:295
  160.5 2.2 copy-start
  162.7 172.6 %collective-permute-start.14 = (bf16[512,768]{1,0:T(8,128)(2,1)S(1)}, bf16[512,768]{1,0:T(8,128)(2,1)}, u32[]{:S(2)}, u32[]{:S(2)}) collective-permute-start(bf16[512,768]{1,0:T(8,128)(2,1)S(1)} %bitcast.157), channel_id=1, source_target_pairs={{0,2},{1,3},{2,0},{3,1},{4,6},{5,7},{6,4},{7,5},{8,10},{9,11},{10,... | collective-permute-start | bytes 2359304 | tf_op jit(solution)/shard_map/ppermute | solution.py:172
  162.8 136.1 %collective-permute-start.12 = (bf16[512,768]{1,0:T(8,128)(2,1)S(1)}, bf16[512,768]{1,0:T(8,128)(2,1)}, u32[]{:S(2)}, u32[]{:S(2)}) collective-permute-start(bf16[512,768]{1,0:T(8,128)(2,1)S(1)} %bitcast.158), channel_id=1, source_target_pairs={{0,1},{1,2},{2,3},{3,0},{4,5},{5,6},{6,7},{7,4},{8,9},{9,10},{10,1... | collective-permute-start | bytes 2359304 | tf_op jit(solution)/shard_map/ppermute | solution.py:172
  174.7 31.5 %collective-permute-start.3 = (bf16[512,192]{1,0:T(8,128)(2,1)}, bf16[512,192]{1,0:T(8,128)(2,1)}, u32[]{:S(2)}, u32[]{:S(2)}) collective-permute-start(bf16[512,192]{1,0:T(8,128)(2,1)} %bitcast.172), channel_id=1, source_target_pairs={{0,1},{1,2},{2,3},{3,0},{4,5},{5,6},{6,7},{7,4},{8,9},{9,10},{10,1... | collective-permute-start | bytes 589832 | tf_op jit(solution)/shard_map/ppermute | solution.py:172
  179.3 49.4 %collective-permute-start.4 = (bf16[512,192]{1,0:T(8,128)(2,1)}, bf16[512,192]{1,0:T(8,128)(2,1)}, u32[]{:S(2)}, u32[]{:S(2)}) collective-permute-start(bf16[512,192]{1,0:T(8,128)(2,1)} %bitcast.171), channel_id=1, source_target_pairs={{0,2},{1,3},{2,0},{3,1},{4,6},{5,7},{6,4},{7,5},{8,10},{9,11},{10,... | collective-permute-start | bytes 589832 | tf_op jit(solution)/shard_map/ppermute | solution.py:172
  182.5 46.2 %collective-permute-start.5 = (bf16[512,192]{1,0:T(8,128)(2,1)}, bf16[512,192]{1,0:T(8,128)(2,1)}, u32[]{:S(2)}, u32[]{:S(2)}) collective-permute-start(bf16[512,192]{1,0:T(8,128)(2,1)} %bitcast.173), channel_id=1, source_target_pairs={{0,3},{1,0},{2,1},{3,2},{4,7},{5,4},{6,5},{7,6},{8,11},{9,8},{10,9... | collective-permute-start | bytes 589832 | tf_op jit(solution)/shard_map/ppermute | solution.py:172
  206.2 140.4 %collective-permute-start.16 = (bf16[512,768]{1,0:T(8,128)(2,1)S(1)}, bf16[512,768]{1,0:T(8,128)(2,1)}, u32[]{:S(2)}, u32[]{:S(2)}) collective-permute-start(bf16[512,768]{1,0:T(8,128)(2,1)S(1)} %bitcast.159), channel_id=1, source_target_pairs={{0,3},{1,0},{2,1},{3,2},{4,7},{5,4},{6,5},{7,6},{8,11},{9,8},{10,9... | collective-permute-start | bytes 2359304 | tf_op jit(solution)/shard_map/ppermute | solution.py:172
  231.0 2.4 copy-start.16
  231.0 2.4 copy-start.21
  239.1 44.2 %copy-start.11 = (bf16[512,768]{1,0:T(8,128)(2,1)S(1)}, bf16[512,768]{1,0:T(8,128)(2,1)}, u32[]{:S(2)}) copy-start(bf16[512,768]{1,0:T(8,128)(2,1)} %get-tuple-element.78) | copy-start | bytes 2359300
  298.9 3.3 copy-start.22
  302.2 2.0 copy-start.24
  304.2 25.9 %copy-start.12 = (bf16[512,768]{1,0:T(8,128)(2,1)S(1)}, bf16[512,768]{1,0:T(8,128)(2,1)}, u32[]{:S(2)}) copy-start(bf16[512,768]{1,0:T(8,128)(2,1)} %get-tuple-element.80) | copy-start | bytes 2359300
  307.5 61.3 %collective-permute-start.13 = (bf16[512,768]{1,0:T(8,128)(2,1)}, bf16[512,768]{1,0:T(8,128)(2,1)}, u32[]{:S(2)}, u32[]{:S(2)}) collective-permute-start(bf16[512,768]{1,0:T(8,128)(2,1)} %get-tuple-element.48), channel_id=1, source_target_pairs={{0,3},{1,0},{2,1},{3,2},{4,7},{5,4},{6,5},{7,6},{8,11},{9,8},{10,9... | collective-permute-start | bytes 2359304 | tf_op jit(solution)/shard_map/ppermute | solution.py:172
  330.1 5.2 copy-start.34
  339.3 2.1 copy-start.9
  341.4 54.2 %collective-permute-start.15 = (bf16[512,768]{1,0:T(8,128)(2,1)}, bf16[512,768]{1,0:T(8,128)(2,1)S(1)}, u32[]{:S(2)}, u32[]{:S(2)}) collective-permute-start(bf16[512,768]{1,0:T(8,128)(2,1)} %get-tuple-element.51), channel_id=1, source_target_pairs={{0,2},{1,3},{2,0},{3,1},{4,6},{5,7},{6,4},{7,5},{8,10},{9,11},{10,... | collective-permute-start | bytes 2359304 | tf_op jit(solution)/shard_map/ppermute | solution.py:172
  350.6 3.1 copy-start.14
  350.7 3.1 copy-start.15
  350.7 3.1 copy-start.17
  350.7 3.0 copy-start.19
  352.7 43.7 %collective-permute-start.17 = (bf16[512,768]{1,0:T(8,128)(2,1)}, bf16[512,768]{1,0:T(8,128)(2,1)}, u32[]{:S(2)}, u32[]{:S(2)}) collective-permute-start(bf16[512,768]{1,0:T(8,128)(2,1)} %get-tuple-element.54), channel_id=1, source_target_pairs={{0,1},{1,2},{2,3},{3,0},{4,5},{5,6},{6,7},{7,4},{8,9},{9,10},{10,1... | collective-permute-start | bytes 2359304 | tf_op jit(solution)/shard_map/ppermute | solution.py:172
  353.7 3.6 copy-start.10
  357.3 6.5 copy-start.35
  365.0 2.9 copy-start.41
  365.3 215.5 %all-reduce.3.cloned.1.call-start = ((), (), s32[]{:S(2)}) async-start(), calls=%async_computation.14 | async-start | bytes 262144
  365.4 2.4 copy-start.23
  402.3 217.8 %reduce-scatter.9.cloned.1.call-start = ((), (), s32[]{:S(2)}) async-start(), calls=%async_computation.12 | async-start | bytes 1327104 | tf_op jit(solution)/shard_map/reduce_scatter | solution.py:295
  409.1 1.2 copy-start.4
  409.1 312.3 %reduce-scatter.7.cloned.1.call-start = ((), (), s32[]{:S(2)}) async-start(), calls=%async_computation.11 | async-start | bytes 1216512 | tf_op jit(solution)/shard_map/reduce_scatter | solution.py:314
  410.4 8.3 %collective-permute-start.6 = (bf16[512,192]{1,0:T(8,128)(2,1)S(1)}, bf16[512,192]{1,0:T(8,128)(2,1)S(1)}, u32[]{:S(2)}, u32[]{:S(2)}) collective-permute-start(bf16[512,192]{1,0:T(8,128)(2,1)S(1)} %get-tuple-element.59), channel_id=1, source_target_pairs={{0,3},{1,0},{2,1},{3,2},{4,7},{5,4},{6,5},{7,6},{8,11},{9,8},{10,9... | collective-permute-start | bytes 589832 | tf_op jit(solution)/shard_map/ppermute | solution.py:172
  410.4 27.3 %collective-permute-start.7 = (bf16[512,192]{1,0:T(8,128)(2,1)S(1)}, bf16[512,192]{1,0:T(8,128)(2,1)S(1)}, u32[]{:S(2)}, u32[]{:S(2)}) collective-permute-start(bf16[512,192]{1,0:T(8,128)(2,1)S(1)} %get-tuple-element.58), channel_id=1, source_target_pairs={{0,2},{1,3},{2,0},{3,1},{4,6},{5,7},{6,4},{7,5},{8,10},{9,11},{10,... | collective-permute-start | bytes 589832 | tf_op jit(solution)/shard_map/ppermute | solution.py:172
  414.0 24.1 %collective-permute-start.8 = (bf16[512,192]{1,0:T(8,128)(2,1)S(1)}, bf16[512,192]{1,0:T(8,128)(2,1)S(1)}, u32[]{:S(2)}, u32[]{:S(2)}) collective-permute-start(bf16[512,192]{1,0:T(8,128)(2,1)S(1)} %get-tuple-element.57), channel_id=1, source_target_pairs={{0,1},{1,2},{2,3},{3,0},{4,5},{5,6},{6,7},{7,4},{8,9},{9,10},{10,1... | collective-permute-start | bytes 589832 | tf_op jit(solution)/shard_map/ppermute | solution.py:172
  418.7 19.4 %copy-start.5 = (bf16[512,192]{1,0:T(8,128)(2,1)}, bf16[512,192]{1,0:T(8,128)(2,1)S(1)}, u32[]{:S(2)}) copy-start(bf16[512,192]{1,0:T(8,128)(2,1)S(1)} %collective-permute-done.6) | copy-start | bytes 589828
  439.5 321.0 %reduce-scatter.11.cloned.1.call-start = ((), (), s32[]{:S(2)}) async-start(), calls=%async_computation.13 | async-start | bytes 1327104 | tf_op jit(solution)/shard_map/reduce_scatter | solution.py:295
  439.6 3.4 copy-start.36
  439.6 3.4 copy-start.42
  442.9 33.7 %collective-permute-start.10 = (bf16[512,768]{1,0:T(8,128)(2,1)}, bf16[512,768]{1,0:T(8,128)(2,1)}, u32[]{:S(2)}, u32[]{:S(2)}) collective-permute-start(bf16[512,768]{1,0:T(8,128)(2,1)} %convolution_convert_fusion.1), channel_id=1, source_target_pairs={{0,2},{1,3},{2,0},{3,1},{4,6},{5,7},{6,4},{7,5},{8,10},{9,11},{10,... | collective-permute-start | bytes 2359304 | tf_op jit(solution)/shard_map/ppermute | solution.py:172
  442.9 1.7 copy-start.44
  444.6 54.3 %collective-permute-start.9 = (bf16[512,768]{1,0:T(8,128)(2,1)}, bf16[512,768]{1,0:T(8,128)(2,1)}, u32[]{:S(2)}, u32[]{:S(2)}) collective-permute-start(bf16[512,768]{1,0:T(8,128)(2,1)} %convolution_convert_fusion.2), channel_id=1, source_target_pairs={{0,3},{1,0},{2,1},{3,2},{4,7},{5,4},{6,5},{7,6},{8,11},{9,8},{10,9... | collective-permute-start | bytes 2359304 | tf_op jit(solution)/shard_map/ppermute | solution.py:172
  444.6 3.7 copy-start.37
  444.6 3.7 copy-start.43
  446.3 52.6 %collective-permute-start.11 = (bf16[512,768]{1,0:T(8,128)(2,1)}, bf16[512,768]{1,0:T(8,128)(2,1)}, u32[]{:S(2)}, u32[]{:S(2)}) collective-permute-start(bf16[512,768]{1,0:T(8,128)(2,1)} %convolution_convert_fusion), channel_id=1, source_target_pairs={{0,1},{1,2},{2,3},{3,0},{4,5},{5,6},{6,7},{7,4},{8,9},{9,10},{10,1... | collective-permute-start | bytes 2359304 | tf_op jit(solution)/shard_map/ppermute | solution.py:172
  453.7 3.2 copy-start.2
  456.9 1.4 copy-start.6
  458.3 1.6 copy-start.8
  461.4 121.2 %all-to-all-start.1 = ((bf16[4,24,576]{2,1,0:T(8,128)(2,1)}), bf16[4,24,576]{2,1,0:T(8,128)(2,1)S(1)}, u32[]{:S(2)}, u32[]{:S(2)}) async-start(bf16[4,24,576]{2,1,0:T(8,128)(2,1)} %bitcast.176), calls=%async_computation.2 | async-start | bytes 245760 | tf_op jit(solution)/shard_map/all_to_all | solution.py:299
  620.1 142.1 %all-to-all-start.2 = ((bf16[4,24,768]{2,1,0:T(8,128)(2,1)}), bf16[4,24,768]{2,1,0:T(8,128)(2,1)S(1)}, u32[]{:S(2)}, u32[]{:S(2)}) async-start(bf16[4,24,768]{2,1,0:T(8,128)(2,1)} %bitcast.175), calls=%async_computation.5 | async-start | bytes 294912 | tf_op jit(solution)/shard_map/all_to_all | solution.py:299
  (9 other events, 8.8 us)
Sparse Core Ops, SparseCore 0:
  10.8 98.7 all-gather.5
  111.5 27.1 all-gather.3
  140.6 24.0 all-gather.7
  365.5 35.8 reduce-scatter.4
  408.3 172.5 all-reduce.2
  584.3 35.8 reduce-scatter.8
  625.2 96.1 reduce-scatter.6
  724.6 35.8 reduce-scatter.10

commit v2 on v1

--- a/solution.py
+++ b/solution.py
@@ -171,6 +171,25 @@
     def send(x, k):
         return lax.ppermute(x, "seq", [(i, (i + k) % n) for i in range(n)])
 
+    def hop(x, pairs):
+        return lax.ppermute(x, "seq", pairs)
+
+    def gather_ring(x, rank):
+        right, left = [x], [x]
+        for t in range(1, n):
+            right.append(hop(right[-1], [(i, i + 1) for i in range(t - 1, n - 1)]))
+            left.append(hop(left[-1], [(i, i - 1) for i in range(1, n - t + 1)]))
+        return [x] + [jnp.where(rank >= k, right[k], left[n - k]) for k in range(1, n)]
+
+    def scatter_ring(parts):
+        right = left = None
+        for t in range(1, n):
+            rising = parts[t] if right is None else parts[t] + right.astype(F32)
+            falling = parts[n - t] if left is None else parts[n - t] + left.astype(F32)
+            right = hop(rising.astype(BF), [(i, i + 1) for i in range(t)])
+            left = hop(falling.astype(BF), [(i, i - 1) for i in range(n - t, n)])
+        return parts[0] + (right.astype(F32) + left.astype(F32))
+
     def body(
         tokens,
         cotangent,
@@ -192,26 +211,34 @@
         rows = w_qkv.shape[0]
         width = d // n
         units = w_down.shape[0]
+        extra = 1
+        while n * (rows + extra) % 16:
+            extra += 1
         tok = tokens.reshape(c, d)
         cot = cotangent.reshape(c, d)
 
-        toks = [tok] + [send(tok, k) for k in range(1, n)]
-
-        full_out = lax.all_gather(w_out, both, axis=0, tiled=True)
+        toks = gather_ring(tok, rank)
+
+        vectors = (b_qkv, b_out, b_up, b_down, gain_attn, shift_attn, gain_mlp, shift_mlp)
+        lengths = [v.shape[0] for v in vectors]
+        total = sum(lengths)
+        pack = jnp.pad(jnp.concatenate(vectors).reshape(1, total), ((0, extra - 1), (0, d - total)))
         qkv_cols = w_qkv.reshape(rows, 3, n, width).transpose(2, 0, 1, 3).reshape(n, rows, 3 * width)
         up_cols = w_up.reshape(rows, nf, n, units).transpose(2, 0, 1, 3).reshape(n, rows, nf * units)
-        cols = jnp.concatenate([qkv_cols, up_cols], axis=2)
-        cols = lax.all_to_all(cols, "seq", split_axis=0, concat_axis=0, tiled=True)
-        cols = lax.all_gather(cols.reshape(n * rows, -1), "fsdp", axis=0, tiled=True)
+        cols = jnp.pad(jnp.concatenate([qkv_cols, up_cols], axis=2), ((0, 0), (0, extra), (0, 0)))
+        same = jnp.broadcast_to(jnp.concatenate([w_out, pack])[None], (n, rows + extra, d))
+        sent = jnp.concatenate([same, cols], axis=2)
+        sent = lax.all_to_all(sent, "seq", split_axis=0, concat_axis=0, tiled=True)
+        first = lax.all_gather(sent[:, :, :d].reshape(-1, d), "fsdp", axis=0, tiled=True)
+        first = first.reshape(nf, n, rows + extra, d)
+        full_out = first[:, :, :rows].reshape(d, d)
+        packs = first[:, :, rows, :total].reshape(nf * n, total)
+        cols = sent[:, :rows, d:].reshape(n * rows, -1)
+        cols = lax.all_gather(cols, "fsdp", axis=0, tiled=True)
         own_qkv = cols[:, : 3 * width]
         own_up = cols[:, 3 * width :]
         own_down = lax.all_gather(w_down, "fsdp", axis=0, tiled=True)
 
-        vectors = (b_qkv, b_out, b_up, b_down, gain_attn, shift_attn, gain_mlp, shift_mlp)
-        lengths = [v.shape[0] for v in vectors]
-        pad = -sum(lengths) % 1024
-        pack = jnp.concatenate(vectors + (jnp.zeros((pad,), BF),)).reshape(-1, 128)
-        packs = lax.all_gather(pack, both, axis=0, tiled=True).reshape(nf * n, -1)
         full = []
         at = 0
         for size in lengths:
@@ -234,7 +261,7 @@
             grad_mixed.append(send(part, k) if k else part)
 
         late_cot, toks[-1] = lax.optimization_barrier((cot, toks[-1]))
-        cots = [cot] + [send(late_cot, k) for k in range(1, n)]
+        cots = gather_ring(late_cot, rank)
 
         hats, ones, twos, scales, projected = [], [], [], [], []
         for k in range(n):
@@ -254,15 +281,14 @@
         tables = [jnp.stack(t) for t in zip(*tables)]
 
         pres, hiddens = [], []
-        mlp_out = None
+        mlp_parts = []
         for k in range(n):
             pre = nn(twos[k], own_up) + own_bias_up
             hidden = jax.nn.gelu(pre, approximate=False).astype(BF)
             pres.append(pre)
             hiddens.append(hidden)
-            part = nn(hidden, own_down)
-            part = send(part.astype(BF), -k).astype(F32) if k else part
-            mlp_out = part if mlp_out is None else mlp_out + part
+            mlp_parts.append(nn(hidden, own_down))
+        mlp_out = scatter_ring(mlp_parts)
 
         mixed, grad_proj, sum_qkv = attend(
             jnp.full((1,), rank, jnp.int32), jnp.stack(projected), jnp.stack(grad_mixed), tables
@@ -295,7 +321,7 @@
             return lax.psum_scatter(grad.astype(BF), "fsdp", scatter_dimension=0, tiled=True)
 
         def to_owners(grad):
-            grad = reduce_rows(grad).reshape(n, rows, -1)
+            grad = reduce_rows(grad).reshape(n, -1, grad.shape[1])
             return lax.all_to_all(grad, "seq", split_axis=0, concat_axis=0, tiled=True).astype(F32)
 
         grad_w_down = reduce_rows(grad_down).astype(F32)
@@ -304,30 +330,25 @@
         )
 
         attn_out = None
-        grad_out = jnp.zeros((n, width, d), F32)
         for k in range(n):
             part = send(mixed[k], -k) if k else mixed[k]
             term = nn(part, out_blocks[k])
             attn_out = term if attn_out is None else attn_out + term
-            grad_out = lax.dynamic_update_index_in_dim(grad_out, tn(part, cot), (rank + k) % n, 0)
         block_out = tok.astype(F32) + attn_out + bias_out + mlp_out + bias_down
-        grad_w_out = lax.psum_scatter(
-            grad_out.reshape(d, d).astype(BF), both, scatter_dimension=0, tiled=True
+        grad_out = reduce_rows(tn(mixed.reshape(n * c, width), cot_all))
+        grad_w_out = lax.ppermute(
+            grad_out, both, [(f * n + s, s * nf + f) for f in range(nf) for s in range(n)]
         ).astype(F32)
 
-        grad_q = None
+        grad_q_parts = []
         sum_gain_one = sum_shift_one = 0.0
         for k in range(n):
             arriving = nt(grad_proj[k], own_qkv)
             sum_gain_one += jnp.sum(arriving * hats[k], axis=0)
             sum_shift_one += jnp.sum(arriving, axis=0)
-            part = arriving * gain_one + incoming[k]
-            part = send(part.astype(BF), -k).astype(F32) if k else part
-            grad_q = part if grad_q is None else grad_q + part
+            grad_q_parts.append(arriving * gain_one + incoming[k])
+        grad_q = scatter_ring(grad_q_parts)
         grad_qkv = tn(one_all, grad_proj.reshape(n * c, -1))
-        grad_w_qkv = (
-            to_owners(grad_qkv).reshape(n, rows, 3, width).transpose(1, 2, 0, 3).reshape(rows, -1)
-        )
         grad_tokens = cot_float + scales[0] * (
             grad_q
             - jnp.mean(grad_q, axis=-1, keepdims=True)
@@ -350,12 +371,15 @@
             sum_gain_two,
             sum_shift_two,
         )
-        packed = jnp.concatenate(
-            [s.reshape(nf * n, -1) for s in sums] + [jnp.zeros((nf * n, pad), F32)], axis=1
-        )
-        packed = lax.psum_scatter(
-            packed.reshape(-1, 128), both, scatter_dimension=0, tiled=True
-        ).reshape(-1)
+        packed = jnp.concatenate([s.reshape(nf * n, -1) for s in sums], axis=1)
+        packed = packed.reshape(nf, n, 1, total)
+        packed = jnp.pad(packed, ((0, 0), (0, 0), (0, extra - 1), (0, 3 * width - total)))
+        tail = jnp.concatenate([grad_qkv.reshape(nf, n, rows, 3 * width), packed], axis=2)
+        tail = to_owners(tail.reshape(-1, 3 * width))
+        grad_w_qkv = (
+            tail[:, :rows].reshape(n, rows, 3, width).transpose(1, 2, 0, 3).reshape(rows, -1)
+        )
+        packed = jnp.sum(tail[:, rows], axis=0)
         grads = []
         at = 0
         for size in lengths:

time: 780 us -> 516 us (0.66)
  waiting for transfers between devices: 368 us -> 138 us
  blocking collectives: 140 us -> 21.4 us
  starting transfers between devices: 50.5 us -> 97.7 us
  other arithmetic: 28.9 us -> 59.1 us
  local copies, waits for them, and re-layouts: 20.6 us -> 45.5 us
  matrix products: 102 us -> 85.5 us
    all_gather x1 -> x0, blocking collectives: 125 us -> none  [body(): packs = lax.all_gather(pack, both, axis=0, tiled=True).reshape(nf * n, -1)]
    ppermute x18 -> x6, waiting for transfers between devices: 121 us -> 16.5 us  [send(): return lax.ppermute(x, 'seq', [(i, (i + k) % n) for i in range(n)])]
    reduce_scatter x1 -> x0, waiting for transfers between devices: 94.8 us -> none  [body(): lax.psum_scatter(grad_out.reshape(d, d).astype(BF), both, scatter_dimensi...]
    ppermute x0 -> x25, waiting for transfers between devices: none -> 77.8 us  [the longest x24 77.8 us: hop(): return lax.ppermute(x, 'seq', pairs)]
    unnamed x9 -> x7, waiting for transfers between devices: 77.8 us -> 0.11 us
    ppermute x0 -> x25, starting transfers between devices: none -> 63 us  [the longest x24 61.6 us: hop(): return lax.ppermute(x, 'seq', pairs)]
    reduce_scatter x3 -> x4, waiting for transfers between devices: 75.2 us -> 38.2 us  [reduce_rows(): lax.psum_scatter(grad.astype(BF), 'fsdp', scatter_dimension=0, tiled=True)]
    ppermute x18 -> x6, starting transfers between devices: 41.3 us -> 14.7 us  [send(): return lax.ppermute(x, 'seq', [(i, (i + k) % n) for i in range(n)])]
  transfers between devices with their start and end apart: 28 -> 40, of which waited for: 11 -> 14; matrix products, arithmetic and copies ran while one was open for 19% -> 35% of each run, Pallas kernels for 6% -> 9%
where the time goes in v2:
time: 516 us; the launch traced here: 507 us
  waiting for transfers between devices  138 us (27%)
  starting transfers between devices  97.7 us (19%)
  matrix products  85.5 us (17%)
  other arithmetic  59.1 us (11%)
  local copies, waits for them, and re-layouts  45.5 us (9%)
  Pallas kernels  44.4 us (9%)
  blocking collectives  21.4 us (4%)
  between operations  16.1 us (3%)
    ppermute x24, waiting for transfers between devices, hop(): return lax.ppermute(x, 'seq', pairs)  77.8 us
    ppermute x24, starting transfers between devices, hop(): return lax.ppermute(x, 'seq', pairs)  61.6 us
    pallas_call x1, Pallas kernels, attend(): pl.pallas_call(kernel, out_shape=(jax.ShapeDtypeStruct((n, c, width), BF)...  44.4 us
    dot_general x16, matrix products, nn(): lax.dot_general(a, b, (((1,), (0,)), ((), ())), preferred_element_type=F32)  43.7 us
    reduce_scatter x4, waiting for transfers between devices, reduce_rows(): lax.psum_scatter(grad.astype(BF), 'fsdp', scatter_dimension=0, tiled=True)  38.2 us
    dot_general x16, matrix products, nt(): lax.dot_general(a, b, (((1,), (1,)), ((), ())), preferred_element_type=F32)  25.8 us
    all_to_all x1, blocking collectives, body(): sent = lax.all_to_all(sent, 'seq', split_axis=0, concat_axis=0, tiled=True)  21.4 us
    all_to_all x2, starting transfers between devices, to_owners(): lax.all_to_all(grad, 'seq', split_axis=0, concat_axis=0, tiled=True)  19.8 us
  transfers between devices with their start and end apart: 40, of which 14 were waited for; matrix products, arithmetic and copies ran while one was open for 35% of the time, Pallas kernels for 9%

profile of v2, /device:TPU:0, one launch (start us, length us, event | category | flops | bytes accessed | tf_op | source)
XLA Modules:
  0.0 507.3 jit_solution(10847598775358326735)
XLA Ops:
  10.4 21.4 %all_to_all.15 = bf16[4,28,2112]{2,1,0:T(8,128)(2,1)S(1)} all-to-all(bf16[4,28,2112]{2,1,0:T(8,128)(2,1)S(1)} %pad_maximum_fusion.6), channel_id=1, replica_groups=mesh['fsdp'=8,'seq'=4] {'seq'}, dimensions={0} | all-to-all | bytes 946176 | tf_op jit(solution)/shard_map/all_to_all | solution.py:231
  33.5 2.4 collective-permute-start
  37.4 3.8 fusion.188
  43.4 8.3 %collective-permute-done = bf16[512,768]{1,0:T(8,128)(2,1)S(1)} collective-permute-done((bf16[512,768]{1,0:T(8,128)(2,1)S(1)}, bf16[512,768]{1,0:T(8,128)(2,1)S(1)}, u32[]{:S(2)}, u32[]{:S(2)}) %collective-permute-start) | collective-permute-done | bytes 786464 | tf_op jit(solution)/shard_map/ppermute | solution.py:175
  53.2 2.6 collective-permute-done.1
  60.4 15.4 %collective-permute-done.2 = bf16[512,768]{1,0:T(8,128)(2,1)} collective-permute-done((bf16[512,768]{1,0:T(8,128)(2,1)S(1)}, bf16[512,768]{1,0:T(8,128)(2,1)}, u32[]{:S(2)}, u32[]{:S(2)}) %collective-permute-start.2) | collective-permute-done | bytes 786464 | tf_op jit(solution)/shard_map/ppermute | solution.py:175
  79.4 5.4 %collective-permute-start.18 = (bf16[512,768]{1,0:T(8,128)(2,1)S(1)}, bf16[512,768]{1,0:T(8,128)(2,1)}, u32[]{:S(2)}, u32[]{:S(2)}) collective-permute-start(bf16[512,768]{1,0:T(8,128)(2,1)S(1)} %bitcast.123), channel_id=1, source_target_pairs={{0,1},{1,2},{2,3},{4,5},{5,6},{6,7},{8,9},{9,10},{10,11},{12,13},{... | collective-permute-start | bytes 2359304 | tf_op jit(solution)/shard_map/ppermute | solution.py:175
  86.9 9.0 %collective-permute-done.3 = bf16[512,768]{1,0:T(8,128)(2,1)S(1)} collective-permute-done((bf16[512,768]{1,0:T(8,128)(2,1)}, bf16[512,768]{1,0:T(8,128)(2,1)S(1)}, u32[]{:S(2)}, u32[]{:S(2)}) %collective-permute-start.3) | collective-permute-done | bytes 786464 | tf_op jit(solution)/shard_map/ppermute | solution.py:175
  96.6 3.3 reshape.1360
  102.1 4.8 fusion.63
  109.9 3.1 maximum_bitcast_fusion
  113.0 4.7 copy.90
  133.0 9.5 %collective-permute-start.7 = (bf16[512,192]{1,0:T(8,128)(2,1)}, bf16[512,192]{1,0:T(8,128)(2,1)}, u32[]{:S(2)}, u32[]{:S(2)}) collective-permute-start(bf16[512,192]{1,0:T(8,128)(2,1)} %bitcast.148), channel_id=1, source_target_pairs={{0,2},{1,3},{2,0},{3,1},{4,6},{5,7},{6,4},{7,5},{8,10},{9,11},{10,... | collective-permute-start | bytes 589832 | tf_op jit(solution)/shard_map/ppermute | solution.py:172
  150.3 16.5 %collective-permute-done.7 = bf16[512,192]{1,0:T(8,128)(2,1)} collective-permute-done((bf16[512,192]{1,0:T(8,128)(2,1)}, bf16[512,192]{1,0:T(8,128)(2,1)}, u32[]{:S(2)}, u32[]{:S(2)}) %collective-permute-start.7) | collective-permute-done | bytes 196640 | tf_op jit(solution)/shard_map/ppermute | solution.py:172
  166.8 2.3 pad_maximum_fusion.2.gm_ref
  172.1 2.1 broadcast_select_fusion.2
  174.2 6.8 %fusion.98 = (bf16[512,768]{1,0:T(8,128)(2,1)}, f32[512,768]{1,0:T(8,128)}) fusion(f32[768]{0:T(1024)S(1)} %copy-done.66, bf16[512,768]{1,0:T(8,128)(2,1)S(1)} %copy-done.31, bf16[768,1344]{1,0:T(8,128)(2,1)} %all-gather.6.cloned.1.call-done), kind=kOutput, calls=%fused_computation.119 | convolution fusion | flops 629932032 | bytes 4328448 | tf_op jit(solution)/shard_map/dot_general | solution.py:34
  181.0 3.8 fusion.265
  184.9 7.3 %collective-permute-start.12 = (bf16[512,768]{1,0:T(8,128)(2,1)}, bf16[512,768]{1,0:T(8,128)(2,1)}, u32[]{:S(2)}, u32[]{:S(2)}) collective-permute-start(bf16[512,768]{1,0:T(8,128)(2,1)} %get-tuple-element.129), channel_id=1, source_target_pairs={{0,1},{4,5},{8,9},{12,13},{16,17},{20,21},{24,25},{28,29}} | collective-permute-start | bytes 2359304 | tf_op jit(solution)/shard_map/ppermute | solution.py:175
  195.7 2.6 pad_maximum_fusion.proj_ref
  198.3 44.4 %attend.1 = (bf16[4,512,192]{2,1,0:T(8,128)(2,1)}, bf16[4,512,576]{2,1,0:T(8,128)(2,1)}, f32[8,576]{1,0:T(8,128)}) custom-call(s32[1]{0:T(128)} %bitcast.1.rank_ref, f32[4,512,576]{2,1,0:T(8,128)} %pad_maximum_fusion.proj_ref, bf16[4,512,192]{2,1,0:T(8,128)(2,1)} %pad_maximum_fusion.2.gm_ref, f32[4,512,128]{2,1,0:T(8,128)} %pad_maximum_fusion.3.c_ref, ...), custom_call_target="tpu_custom_call" | custom-call | flops 19327352832 | bytes 16777216 | tf_op jit(solution)/shard_map/attend/pallas_call | solution.py:146
  242.7 2.0 slice_bitcast_fusion.2
  245.4 6.5 %convolution_convert_fusion = bf16[8,4,24,576]{3,2,1,0:T(8,128)(2,1)} fusion(bf16[8,4,24,2048]{3,2,1,0:T(8,128)(2,1)} %bitcast.138, bf16[2048,576,1,1]{1,0,3,2:T(8,128)(2,1)} %bitcast.141), kind=kOutput, calls=%fused_computation.226 | convolution fusion | flops 1812381696 | bytes 6389760 | tf_op jit(solution)/shard_map/dot_general | solution.py:165
  253.6 2.0 fusion.174
  255.6 4.1 fusion.95
  259.8 4.3 fusion.92
  264.1 4.1 fusion.89
  271.3 2.0 fusion.219
  273.4 2.0 fusion.266
  276.7 2.5 fusion.199
  279.8 3.8 collective-permute-start.9
  283.6 2.5 fusion.202
  286.1 2.5 fusion.205
  291.3 2.1 fusion.181
  293.5 2.7 collective-permute-start.24
  298.6 3.6 add_convert_fusion.7
  302.2 2.2 collective-permute-start.13
  304.4 9.5 %collective-permute-done.24 = bf16[512,768]{1,0:T(8,128)(2,1)S(1)} collective-permute-done((bf16[512,768]{1,0:T(8,128)(2,1)S(1)}, bf16[512,768]{1,0:T(8,128)(2,1)S(1)}, u32[]{:S(2)}, u32[]{:S(2)}) %collective-permute-start.24) | collective-permute-done | bytes 786464 | tf_op jit(solution)/shard_map/ppermute | solution.py:175
  313.9 2.4 add_convert_fusion.3
  316.3 5.3 %collective-permute-start.25 = (bf16[512,768]{1,0:T(8,128)(2,1)}, bf16[512,768]{1,0:T(8,128)(2,1)}, u32[]{:S(2)}, u32[]{:S(2)}) collective-permute-start(bf16[512,768]{1,0:T(8,128)(2,1)} %get-tuple-element.119), channel_id=1, source_target_pairs={{0,1},{1,2},{4,5},{5,6},{8,9},{9,10},{12,13},{13,14},{16,17},{17,1... | collective-permute-start | bytes 2359304 | tf_op jit(solution)/shard_map/ppermute | solution.py:175
  321.6 3.8 fusion.154
  325.5 2.6 fusion.217
  328.1 2.7 collective-permute-done.13
  330.9 2.6 add_convert_fusion.6
  335.0 8.3 %collective-permute-done.25 = bf16[512,768]{1,0:T(8,128)(2,1)} collective-permute-done((bf16[512,768]{1,0:T(8,128)(2,1)}, bf16[512,768]{1,0:T(8,128)(2,1)}, u32[]{:S(2)}, u32[]{:S(2)}) %collective-permute-start.25) | collective-permute-done | bytes 786464 | tf_op jit(solution)/shard_map/ppermute | solution.py:175
  343.3 4.2 fusion.258
  349.1 2.5 fusion.208
  351.7 2.8 add_convert_fusion.5
  356.1 3.5 fusion.257
  361.1 1.9 convolution_convert_fusion.1
  363.1 4.7 collective-permute-start.14
  367.9 8.9 %collective-permute-start.26 = (bf16[512,768]{1,0:T(8,128)(2,1)}, bf16[512,768]{1,0:T(8,128)(2,1)}, u32[]{:S(2)}, u32[]{:S(2)}) collective-permute-start(bf16[512,768]{1,0:T(8,128)(2,1)} %get-tuple-element.61), channel_id=1, source_target_pairs={{0,1},{1,2},{2,3},{4,5},{5,6},{6,7},{8,9},{9,10},{10,11},{12,13},{... | collective-permute-start | bytes 2359304 | tf_op jit(solution)/shard_map/ppermute | solution.py:175
  376.8 2.9 add_convert_fusion.4
  381.1 3.0 fusion.255
  385.9 3.8 fusion.151
  389.8 6.9 %collective-permute-done.26 = bf16[512,768]{1,0:T(8,128)(2,1)} collective-permute-done((bf16[512,768]{1,0:T(8,128)(2,1)}, bf16[512,768]{1,0:T(8,128)(2,1)}, u32[]{:S(2)}, u32[]{:S(2)}) %collective-permute-start.26) | collective-permute-done | bytes 786464 | tf_op jit(solution)/shard_map/ppermute | solution.py:175
  397.1 14.6 %collective-permute-done.29 = bf16[512,768]{1,0:T(8,128)(2,1)} collective-permute-done((bf16[512,768]{1,0:T(8,128)(2,1)}, bf16[512,768]{1,0:T(8,128)(2,1)}, u32[]{:S(2)}, u32[]{:S(2)}) %collective-permute-start.29) | collective-permute-done | bytes 786464 | tf_op jit(solution)/shard_map/ppermute | solution.py:175
  411.8 7.7 %fusion.256 = (f32[768]{0:T(1024)S(1)}, f32[768]{0:T(1024)S(1)}, f32[512]{0:T(512)}, f32[512]{0:T(512)}, f32[512,768]{1,0:T(8,128)}, /*index=5*/f32[768]{0:T(1024)S(1)}, f32[768]{0:T(1024)S(1)}, bf16[1,512,768]{2,1,0:T(8,128)(2,1)}) fusion(f32[512,768]{1,0:T(8,128)} %fusion.219, f32[512]{0:T(512)S(1)} %copy-done.52, f32[512]{0:T(512)S(1)} %broadcast_multiply_fusion.5, ...), kind=kLoop, calls=%fused_computation.398 | loop fusion | flops 12185600 | bytes 17334272 | tf_op jit(solution)/shard_map/reduce_sum | solution.py:311
  423.1 15.2 %all-to-all-start.2 = ((bf16[4,24,768]{2,1,0:T(8,128)(2,1)}), bf16[4,24,768]{2,1,0:T(8,128)(2,1)}, u32[]{:S(2)}, u32[]{:S(2)}) async-start(bf16[4,24,768]{2,1,0:T(8,128)(2,1)} %bitcast.150), calls=%async_computation.5 | async-start | bytes 294912 | tf_op jit(solution)/shard_map/all_to_all | solution.py:325
  440.4 4.3 reduce-scatter.11.cloned.1.call-done
  448.5 2.1 reshape.1385
  450.5 33.8 %reduce-scatter.5.cloned.1.call-done = bf16[112,576]{1,0:T(8,128)(2,1)} async-done(((bf16[896,576]{1,0:T(8,128)(2,1)}), bf16[112,576]{1,0:T(8,128)(2,1)}) %reduce-scatter.5.cloned.1.call-update) | async-done | bytes 129040 | tf_op jit(solution)/shard_map/reduce_scatter | solution.py:321
  486.0 4.6 all-to-all-start.1
  492.1 4.9 all-to-all-done.1
  (345 shorter events, 93.0 us)
Async XLA Ops:
  7.3 89.3 %all-gather.4.cloned.1.call-start = ((), (), s32[]{:S(2)}) async-start(), calls=%async_computation.7 | async-start | bytes 1548288 | tf_op jit(solution)/shard_map/all_gather | solution.py:232
  10.4 23.1 %copy-start.1 = (bf16[1,512,768]{2,1,0:T(8,128)(2,1)S(1)}, bf16[1,512,768]{2,1,0:T(8,128)(2,1)}, u32[]{:S(2)}) copy-start(bf16[1,512,768]{2,1,0:T(8,128)(2,1)} %param.14) | copy-start | bytes 2359300
  32.6 141.6 %all-gather.6.cloned.1.call-start = ((), (), s32[]{:S(2)}) async-start(), calls=%async_computation.8 | async-start | bytes 2433024 | tf_op jit(solution)/shard_map/all_gather | solution.py:237
  33.4 147.6 %all-gather.8.cloned.1.call-start = ((), (), s32[]{:S(2)}) async-start(), calls=%async_computation.9 | async-start | bytes 1327104 | tf_op jit(solution)/shard_map/all_gather | solution.py:240
  33.5 18.2 %collective-permute-start = (bf16[512,768]{1,0:T(8,128)(2,1)S(1)}, bf16[512,768]{1,0:T(8,128)(2,1)S(1)}, u32[]{:S(2)}, u32[]{:S(2)}) collective-permute-start(bf16[512,768]{1,0:T(8,128)(2,1)S(1)} %bitcast.128), channel_id=1, source_target_pairs={{0,1},{1,2},{2,3},{4,5},{5,6},{6,7},{8,9},{9,10},{10,11},{12,13},{... | collective-permute-start | bytes 2359304 | tf_op jit(solution)/shard_map/ppermute | solution.py:175
  35.9 19.9 %collective-permute-start.1 = (bf16[512,768]{1,0:T(8,128)(2,1)S(1)}, bf16[512,768]{1,0:T(8,128)(2,1)S(1)}, u32[]{:S(2)}, u32[]{:S(2)}) collective-permute-start(bf16[512,768]{1,0:T(8,128)(2,1)S(1)} %bitcast.129), channel_id=1, source_target_pairs={{1,0},{2,1},{3,2},{5,4},{6,5},{7,6},{9,8},{10,9},{11,10},{13,12},{... | collective-permute-start | bytes 2359304 | tf_op jit(solution)/shard_map/ppermute | solution.py:175
  37.2 385.9 %reduce-scatter.9.cloned.1.call-start = ((), (), s32[]{:S(2)}) async-start(), calls=%async_computation.12 | async-start | bytes 1327104 | tf_op jit(solution)/shard_map/reduce_scatter | solution.py:321
  43.4 14.8 %copy-start = (bf16[1,512,768]{2,1,0:T(8,128)(2,1)S(1)}, bf16[1,512,768]{2,1,0:T(8,128)(2,1)}, u32[]{:S(2)}) copy-start(bf16[1,512,768]{2,1,0:T(8,128)(2,1)} %param.15) | copy-start | bytes 2359300
  51.7 8.0 %collective-permute-start.4 = (bf16[512,768]{1,0:T(8,128)(2,1)S(1)}, bf16[512,768]{1,0:T(8,128)(2,1)}, u32[]{:S(2)}, u32[]{:S(2)}) collective-permute-start(bf16[512,768]{1,0:T(8,128)(2,1)S(1)} %collective-permute-done), channel_id=1, source_target_pairs={{1,2},{2,3},{5,6},{6,7},{9,10},{10,11},{13,14},{14,15},{17,18},{18... | collective-permute-start | bytes 2359304 | tf_op jit(solution)/shard_map/ppermute | solution.py:175
  55.8 19.9 %collective-permute-start.2 = (bf16[512,768]{1,0:T(8,128)(2,1)S(1)}, bf16[512,768]{1,0:T(8,128)(2,1)}, u32[]{:S(2)}, u32[]{:S(2)}) collective-permute-start(bf16[512,768]{1,0:T(8,128)(2,1)S(1)} %collective-permute-done.1), channel_id=1, source_target_pairs={{1,0},{2,1},{5,4},{6,5},{9,8},{10,9},{13,12},{14,13},{17,16},{18,1... | collective-permute-start | bytes 2359304 | tf_op jit(solution)/shard_map/ppermute | solution.py:175
  59.6 42.4 %copy-start.51 = (f32[512]{0:T(512)}, f32[512]{0:T(512)S(1)}, u32[]{:S(2)}) copy-start(f32[512]{0:T(512)S(1)} %add_rsqrt_fusion.3) | copy-start | bytes 6148
  59.6 19.4 %collective-permute-start.5 = (bf16[512,768]{1,0:T(8,128)(2,1)}, bf16[512,768]{1,0:T(8,128)(2,1)S(1)}, u32[]{:S(2)}, u32[]{:S(2)}) collective-permute-start(bf16[512,768]{1,0:T(8,128)(2,1)} %collective-permute-done.4), channel_id=1, source_target_pairs={{2,3},{6,7},{10,11},{14,15},{18,19},{22,23},{26,27},{30,31}} | collective-permute-start | bytes 2359304 | tf_op jit(solution)/shard_map/ppermute | solution.py:175
  75.7 20.2 %collective-permute-start.3 = (bf16[512,768]{1,0:T(8,128)(2,1)}, bf16[512,768]{1,0:T(8,128)(2,1)S(1)}, u32[]{:S(2)}, u32[]{:S(2)}) collective-permute-start(bf16[512,768]{1,0:T(8,128)(2,1)} %collective-permute-done.2), channel_id=1, source_target_pairs={{1,0},{5,4},{9,8},{13,12},{17,16},{21,20},{25,24},{29,28}} | collective-permute-start | bytes 2359304 | tf_op jit(solution)/shard_map/ppermute | solution.py:175
  78.6 23.4 %copy-start.49 = (f32[512]{0:T(512)}, f32[512]{0:T(512)S(1)}, u32[]{:S(2)}) copy-start(f32[512]{0:T(512)S(1)} %broadcast_multiply_fusion.3) | copy-start | bytes 6148
  79.0 23.1 %copy-start.56 = (f32[512]{0:T(512)}, f32[512]{0:T(512)S(1)}, u32[]{:S(2)}) copy-start(f32[512]{0:T(512)S(1)} %add_rsqrt_fusion.1) | copy-start | bytes 6148
  79.0 16.9 %copy-start.43 = (bf16[512,768]{1,0:T(8,128)(2,1)S(1)}, bf16[512,768]{1,0:T(8,128)(2,1)}, u32[]{:S(2)}) copy-start(bf16[512,768]{1,0:T(8,128)(2,1)} %copy-done.42) | copy-start | bytes 2359300
  79.4 22.6 %copy-start.6 = (bf16[512,768]{1,0:T(8,128)(2,1)}, bf16[512,768]{1,0:T(8,128)(2,1)S(1)}, u32[]{:S(2)}) copy-start(bf16[512,768]{1,0:T(8,128)(2,1)S(1)} %broadcast_select_fusion.1) | copy-start | bytes 2359300
  79.4 47.8 %collective-permute-start.18 = (bf16[512,768]{1,0:T(8,128)(2,1)S(1)}, bf16[512,768]{1,0:T(8,128)(2,1)}, u32[]{:S(2)}, u32[]{:S(2)}) collective-permute-start(bf16[512,768]{1,0:T(8,128)(2,1)S(1)} %bitcast.123), channel_id=1, source_target_pairs={{0,1},{1,2},{2,3},{4,5},{5,6},{6,7},{8,9},{9,10},{10,11},{12,13},{... | collective-permute-start | bytes 2359304 | tf_op jit(solution)/shard_map/ppermute | solution.py:175
  84.8 44.0 %collective-permute-start.21 = (bf16[512,768]{1,0:T(8,128)(2,1)S(1)}, bf16[512,768]{1,0:T(8,128)(2,1)}, u32[]{:S(2)}, u32[]{:S(2)}) collective-permute-start(bf16[512,768]{1,0:T(8,128)(2,1)S(1)} %bitcast.124), channel_id=1, source_target_pairs={{1,0},{2,1},{3,2},{5,4},{6,5},{7,6},{9,8},{10,9},{11,10},{13,12},{... | collective-permute-start | bytes 2359304 | tf_op jit(solution)/shard_map/ppermute | solution.py:175
  86.5 15.6 %copy-start.58 = (f32[512]{0:T(512)}, f32[512]{0:T(512)S(1)}, u32[]{:S(2)}) copy-start(f32[512]{0:T(512)S(1)} %broadcast_multiply_fusion.2) | copy-start | bytes 6148
  86.8 15.2 %copy-start.62 = (f32[512]{0:T(512)}, f32[512]{0:T(512)S(1)}, u32[]{:S(2)}) copy-start(f32[512]{0:T(512)S(1)} %add_rsqrt_fusion) | copy-start | bytes 6148
  107.8 37.5 %copy-start.12 = (bf16[8,4,24,768]{3,2,1,0:T(8,128)(2,1)}, bf16[8,4,24,768]{3,2,1,0:T(8,128)(2,1)S(1)}, u32[]{:S(2)}) copy-start(bf16[8,4,24,768]{3,2,1,0:T(8,128)(2,1)S(1)} %slice.135) | copy-start | bytes 3538948
  125.9 24.4 %collective-permute-start.6 = (bf16[512,192]{1,0:T(8,128)(2,1)}, bf16[512,192]{1,0:T(8,128)(2,1)}, u32[]{:S(2)}, u32[]{:S(2)}) collective-permute-start(bf16[512,192]{1,0:T(8,128)(2,1)} %bitcast.147), channel_id=1, source_target_pairs={{0,1},{1,2},{2,3},{3,0},{4,5},{5,6},{6,7},{7,4},{8,9},{9,10},{10,1... | collective-permute-start | bytes 589832 | tf_op jit(solution)/shard_map/ppermute | solution.py:172
  127.3 41.9 %collective-permute-start.19 = (bf16[512,768]{1,0:T(8,128)(2,1)}, bf16[512,768]{1,0:T(8,128)(2,1)}, u32[]{:S(2)}, u32[]{:S(2)}) collective-permute-start(bf16[512,768]{1,0:T(8,128)(2,1)} %collective-permute-done.18), channel_id=1, source_target_pairs={{1,2},{2,3},{5,6},{6,7},{9,10},{10,11},{13,14},{14,15},{17,18},{18... | collective-permute-start | bytes 2359304 | tf_op jit(solution)/shard_map/ppermute | solution.py:175
  128.8 42.0 %collective-permute-start.22 = (bf16[512,768]{1,0:T(8,128)(2,1)}, bf16[512,768]{1,0:T(8,128)(2,1)}, u32[]{:S(2)}, u32[]{:S(2)}) collective-permute-start(bf16[512,768]{1,0:T(8,128)(2,1)} %collective-permute-done.21), channel_id=1, source_target_pairs={{1,0},{2,1},{5,4},{6,5},{9,8},{10,9},{13,12},{14,13},{17,16},{18,1... | collective-permute-start | bytes 2359304 | tf_op jit(solution)/shard_map/ppermute | solution.py:175
  133.0 33.8 %collective-permute-start.7 = (bf16[512,192]{1,0:T(8,128)(2,1)}, bf16[512,192]{1,0:T(8,128)(2,1)}, u32[]{:S(2)}, u32[]{:S(2)}) collective-permute-start(bf16[512,192]{1,0:T(8,128)(2,1)} %bitcast.148), channel_id=1, source_target_pairs={{0,2},{1,3},{2,0},{3,1},{4,6},{5,7},{6,4},{7,5},{8,10},{9,11},{10,... | collective-permute-start | bytes 589832 | tf_op jit(solution)/shard_map/ppermute | solution.py:172
  145.3 21.5 %collective-permute-start.8 = (bf16[512,192]{1,0:T(8,128)(2,1)}, bf16[512,192]{1,0:T(8,128)(2,1)}, u32[]{:S(2)}, u32[]{:S(2)}) collective-permute-start(bf16[512,192]{1,0:T(8,128)(2,1)} %bitcast.149), channel_id=1, source_target_pairs={{0,3},{1,0},{2,1},{3,2},{4,7},{5,4},{6,5},{7,6},{8,11},{9,8},{10,9... | collective-permute-start | bytes 589832 | tf_op jit(solution)/shard_map/ppermute | solution.py:172
  169.1 127.0 %collective-permute-start.20 = (bf16[512,768]{1,0:T(8,128)(2,1)}, bf16[512,768]{1,0:T(8,128)(2,1)}, u32[]{:S(2)}, u32[]{:S(2)}) collective-permute-start(bf16[512,768]{1,0:T(8,128)(2,1)} %collective-permute-done.19), channel_id=1, source_target_pairs={{2,3},{6,7},{10,11},{14,15},{18,19},{22,23},{26,27},{30,31}} | collective-permute-start | bytes 2359304 | tf_op jit(solution)/shard_map/ppermute | solution.py:175
  170.8 117.7 %collective-permute-start.23 = (bf16[512,768]{1,0:T(8,128)(2,1)}, bf16[512,768]{1,0:T(8,128)(2,1)}, u32[]{:S(2)}, u32[]{:S(2)}) collective-permute-start(bf16[512,768]{1,0:T(8,128)(2,1)} %collective-permute-done.22), channel_id=1, source_target_pairs={{1,0},{5,4},{9,8},{13,12},{17,16},{21,20},{25,24},{29,28}} | collective-permute-start | bytes 2359304 | tf_op jit(solution)/shard_map/ppermute | solution.py:175
  184.9 113.7 %collective-permute-start.12 = (bf16[512,768]{1,0:T(8,128)(2,1)}, bf16[512,768]{1,0:T(8,128)(2,1)}, u32[]{:S(2)}, u32[]{:S(2)}) collective-permute-start(bf16[512,768]{1,0:T(8,128)(2,1)} %get-tuple-element.129), channel_id=1, source_target_pairs={{0,1},{4,5},{8,9},{12,13},{16,17},{20,21},{24,25},{28,29}} | collective-permute-start | bytes 2359304 | tf_op jit(solution)/shard_map/ppermute | solution.py:175
  244.7 34.4 %collective-permute-start.11 = (bf16[512,192]{1,0:T(8,128)(2,1)}, bf16[512,192]{1,0:T(8,128)(2,1)S(1)}, u32[]{:S(2)}, u32[]{:S(2)}) collective-permute-start(bf16[512,192]{1,0:T(8,128)(2,1)} %get-tuple-element.67), channel_id=1, source_target_pairs={{0,1},{1,2},{2,3},{3,0},{4,5},{5,6},{6,7},{7,4},{8,9},{9,10},{10,1... | collective-permute-start | bytes 589832 | tf_op jit(solution)/shard_map/ppermute | solution.py:172
  244.8 41.3 %collective-permute-start.10 = (bf16[512,192]{1,0:T(8,128)(2,1)}, bf16[512,192]{1,0:T(8,128)(2,1)}, u32[]{:S(2)}, u32[]{:S(2)}) collective-permute-start(bf16[512,192]{1,0:T(8,128)(2,1)} %get-tuple-element.68), channel_id=1, source_target_pairs={{0,2},{1,3},{2,0},{3,1},{4,6},{5,7},{6,4},{7,5},{8,10},{9,11},{10,... | collective-permute-start | bytes 589832 | tf_op jit(solution)/shard_map/ppermute | solution.py:172
  253.6 60.3 %copy-start.2 = (f32[512,768]{1,0:T(8,128)}, f32[512,768]{1,0:T(8,128)S(1)}, u32[]{:S(2)}) copy-start(f32[512,768]{1,0:T(8,128)S(1)} %fusion.170) | copy-start | bytes 4718596
  259.7 38.8 %copy-start.34 = (bf16[512,768]{1,0:T(8,128)(2,1)}, bf16[512,768]{1,0:T(8,128)(2,1)S(1)}, u32[]{:S(2)}) copy-start(bf16[512,768]{1,0:T(8,128)(2,1)S(1)} %get-tuple-element.125) | copy-start | bytes 2359300
  279.8 69.3 %collective-permute-start.9 = (bf16[512,192]{1,0:T(8,128)(2,1)}, bf16[512,192]{1,0:T(8,128)(2,1)S(1)}, u32[]{:S(2)}, u32[]{:S(2)}) collective-permute-start(bf16[512,192]{1,0:T(8,128)(2,1)} %get-tuple-element.66), channel_id=1, source_target_pairs={{0,3},{1,0},{2,1},{3,2},{4,7},{5,4},{6,5},{7,6},{8,11},{9,8},{10,9... | collective-permute-start | bytes 589832 | tf_op jit(solution)/shard_map/ppermute | solution.py:172
  293.5 20.4 %collective-permute-start.24 = (bf16[512,768]{1,0:T(8,128)(2,1)S(1)}, bf16[512,768]{1,0:T(8,128)(2,1)S(1)}, u32[]{:S(2)}, u32[]{:S(2)}) collective-permute-start(bf16[512,768]{1,0:T(8,128)(2,1)S(1)} %get-tuple-element.117), channel_id=1, source_target_pairs={{0,1},{4,5},{8,9},{12,13},{16,17},{20,21},{24,25},{28,29}} | collective-permute-start | bytes 2359304 | tf_op jit(solution)/shard_map/ppermute | solution.py:175
  298.5 23.1 %copy-start.81 = (bf16[512,768]{1,0:T(8,128)(2,1)}, bf16[512,768]{1,0:T(8,128)(2,1)S(1)}, u32[]{:S(2)}) copy-start(bf16[512,768]{1,0:T(8,128)(2,1)S(1)} %get-tuple-element.134) | copy-start | bytes 2359300
  302.2 28.7 %collective-permute-start.13 = (bf16[512,768]{1,0:T(8,128)(2,1)}, bf16[512,768]{1,0:T(8,128)(2,1)}, u32[]{:S(2)}, u32[]{:S(2)}) collective-permute-start(bf16[512,768]{1,0:T(8,128)(2,1)} %get-tuple-element.131), channel_id=1, source_target_pairs={{0,1},{1,2},{4,5},{5,6},{8,9},{9,10},{12,13},{13,14},{16,17},{17,1... | collective-permute-start | bytes 2359304 | tf_op jit(solution)/shard_map/ppermute | solution.py:175
  316.3 27.0 %collective-permute-start.25 = (bf16[512,768]{1,0:T(8,128)(2,1)}, bf16[512,768]{1,0:T(8,128)(2,1)}, u32[]{:S(2)}, u32[]{:S(2)}) collective-permute-start(bf16[512,768]{1,0:T(8,128)(2,1)} %get-tuple-element.119), channel_id=1, source_target_pairs={{0,1},{1,2},{4,5},{5,6},{8,9},{9,10},{12,13},{13,14},{16,17},{17,1... | collective-permute-start | bytes 2359304 | tf_op jit(solution)/shard_map/ppermute | solution.py:175
  325.4 112.9 %reduce-scatter.7.cloned.1.call-start = ((), (), s32[]{:S(2)}) async-start(), calls=%async_computation.11 | async-start | bytes 331776 | tf_op jit(solution)/shard_map/reduce_scatter | solution.py:321
  328.1 15.2 %copy-start.7 = (bf16[512,768]{1,0:T(8,128)(2,1)S(1)}, bf16[512,768]{1,0:T(8,128)(2,1)}, u32[]{:S(2)}) copy-start(bf16[512,768]{1,0:T(8,128)(2,1)} %copy-done.6) | copy-start | bytes 2359300
  328.1 15.2 %copy-start.59 = (f32[512]{0:T(512)S(1)}, f32[512]{0:T(512)}, u32[]{:S(2)}) copy-start(f32[512]{0:T(512)} %copy-done.58) | copy-start | bytes 6148
  328.1 15.2 %copy-start.63 = (f32[512]{0:T(512)S(1)}, f32[512]{0:T(512)}, u32[]{:S(2)}) copy-start(f32[512]{0:T(512)} %copy-done.62) | copy-start | bytes 6148
  333.5 18.2 %collective-permute-start.15 = (bf16[512,768]{1,0:T(8,128)(2,1)}, bf16[512,768]{1,0:T(8,128)(2,1)}, u32[]{:S(2)}, u32[]{:S(2)}) collective-permute-start(bf16[512,768]{1,0:T(8,128)(2,1)} %get-tuple-element.65), channel_id=1, source_target_pairs={{3,2},{7,6},{11,10},{15,14},{19,18},{23,22},{27,26},{31,30}} | collective-permute-start | bytes 2359304 | tf_op jit(solution)/shard_map/ppermute | solution.py:175
  347.5 8.5 %collective-permute-start.27 = (bf16[512,768]{1,0:T(8,128)(2,1)}, bf16[512,768]{1,0:T(8,128)(2,1)}, u32[]{:S(2)}, u32[]{:S(2)}) collective-permute-start(bf16[512,768]{1,0:T(8,128)(2,1)} %get-tuple-element.60), channel_id=1, source_target_pairs={{3,2},{7,6},{11,10},{15,14},{19,18},{23,22},{27,26},{31,30}} | collective-permute-start | bytes 2359304 | tf_op jit(solution)/shard_map/ppermute | solution.py:175
  354.5 22.3 %collective-permute-start.16 = (bf16[512,768]{1,0:T(8,128)(2,1)}, bf16[512,768]{1,0:T(8,128)(2,1)}, u32[]{:S(2)}, u32[]{:S(2)}) collective-permute-start(bf16[512,768]{1,0:T(8,128)(2,1)} %add_convert_fusion.5), channel_id=1, source_target_pairs={{2,1},{3,2},{6,5},{7,6},{10,9},{11,10},{14,13},{15,14},{18,17},{19... | collective-permute-start | bytes 2359304 | tf_op jit(solution)/shard_map/ppermute | solution.py:175
  359.6 21.5 %collective-permute-start.28 = (bf16[512,768]{1,0:T(8,128)(2,1)}, bf16[512,768]{1,0:T(8,128)(2,1)}, u32[]{:S(2)}, u32[]{:S(2)}) collective-permute-start(bf16[512,768]{1,0:T(8,128)(2,1)} %get-tuple-element.57), channel_id=1, source_target_pairs={{2,1},{3,2},{6,5},{7,6},{10,9},{11,10},{14,13},{15,14},{18,17},{19... | collective-permute-start | bytes 2359304 | tf_op jit(solution)/shard_map/ppermute | solution.py:175
  363.1 81.6 %reduce-scatter.11.cloned.1.call-start = ((), (), s32[]{:S(2)}) async-start(), calls=%async_computation.13 | async-start | bytes 1327104 | tf_op jit(solution)/shard_map/reduce_scatter | solution.py:321
  363.1 26.6 %collective-permute-start.14 = (bf16[512,768]{1,0:T(8,128)(2,1)}, bf16[512,768]{1,0:T(8,128)(2,1)}, u32[]{:S(2)}, u32[]{:S(2)}) collective-permute-start(bf16[512,768]{1,0:T(8,128)(2,1)} %get-tuple-element.64), channel_id=1, source_target_pairs={{0,1},{1,2},{2,3},{4,5},{5,6},{6,7},{8,9},{9,10},{10,11},{12,13},{... | collective-permute-start | bytes 2359304 | tf_op jit(solution)/shard_map/ppermute | solution.py:175
  367.9 28.8 %collective-permute-start.26 = (bf16[512,768]{1,0:T(8,128)(2,1)}, bf16[512,768]{1,0:T(8,128)(2,1)}, u32[]{:S(2)}, u32[]{:S(2)}) collective-permute-start(bf16[512,768]{1,0:T(8,128)(2,1)} %get-tuple-element.61), channel_id=1, source_target_pairs={{0,1},{1,2},{2,3},{4,5},{5,6},{6,7},{8,9},{9,10},{10,11},{12,13},{... | collective-permute-start | bytes 2359304 | tf_op jit(solution)/shard_map/ppermute | solution.py:175
  379.7 17.4 %collective-permute-start.17 = (bf16[512,768]{1,0:T(8,128)(2,1)}, bf16[512,768]{1,0:T(8,128)(2,1)}, u32[]{:S(2)}, u32[]{:S(2)}) collective-permute-start(bf16[512,768]{1,0:T(8,128)(2,1)} %add_convert_fusion.4), channel_id=1, source_target_pairs={{1,0},{2,1},{3,2},{5,4},{6,5},{7,6},{9,8},{10,9},{11,10},{13,12},{... | collective-permute-start | bytes 2359304 | tf_op jit(solution)/shard_map/ppermute | solution.py:175
  384.1 27.6 %copy-start.52 = (f32[512]{0:T(512)S(1)}, f32[512]{0:T(512)}, u32[]{:S(2)}) copy-start(f32[512]{0:T(512)} %copy-done.51) | copy-start | bytes 6148
  384.1 27.6 %copy-start.60 = (f32[768]{0:T(1024)S(1)}, f32[768]{0:T(1024)}, u32[]{:S(2)}) copy-start(f32[768]{0:T(1024)} %reshape.1378) | copy-start | bytes 9220
  384.1 27.6 %copy-start.61 = (f32[768]{0:T(1024)S(1)}, f32[768]{0:T(1024)}, u32[]{:S(2)}) copy-start(f32[768]{0:T(1024)} %reshape.1382) | copy-start | bytes 9220
  384.1 27.6 %collective-permute-start.29 = (bf16[512,768]{1,0:T(8,128)(2,1)}, bf16[512,768]{1,0:T(8,128)(2,1)}, u32[]{:S(2)}, u32[]{:S(2)}) collective-permute-start(bf16[512,768]{1,0:T(8,128)(2,1)} %get-tuple-element.54), channel_id=1, source_target_pairs={{1,0},{2,1},{3,2},{5,4},{6,5},{7,6},{9,8},{10,9},{11,10},{13,12},{... | collective-permute-start | bytes 2359304 | tf_op jit(solution)/shard_map/ppermute | solution.py:175
  385.9 25.9 %copy-start.15 = (f32[512,768]{1,0:T(8,128)S(1)}, f32[512,768]{1,0:T(8,128)}, u32[]{:S(2)}) copy-start(f32[512,768]{1,0:T(8,128)} %fusion.174) | copy-start | bytes 4718596
  389.7 94.7 %reduce-scatter.5.cloned.1.call-start = ((), (), s32[]{:S(2)}) async-start(), calls=%async_computation.10 | async-start | bytes 1290240 | tf_op jit(solution)/shard_map/reduce_scatter | solution.py:321
  389.8 30.1 %copy-start.47 = (bf16[8,4,1,24]{3,2,1,0:T(2,128)(2,1)S(1)}, bf16[8,4,1,24]{3,2,1,0:T(2,128)(2,1)}, u32[]{:S(2)}) copy-start(bf16[8,4,1,24]{3,2,1,0:T(2,128)(2,1)} %reshape.1390) | copy-start | bytes 4612
  423.1 27.5 %copy-start.65 = (f32[512]{0:T(512)S(1)}, f32[512]{0:T(512)}, u32[]{:S(2)}) copy-start(f32[512]{0:T(512)} %get-tuple-element.49) | copy-start | bytes 6148
  423.1 27.5 %copy-start.64 = (f32[512]{0:T(512)S(1)}, f32[512]{0:T(512)}, u32[]{:S(2)}) copy-start(f32[512]{0:T(512)} %get-tuple-element.50) | copy-start | bytes 6148
  423.1 23.2 %all-to-all-start.2 = ((bf16[4,24,768]{2,1,0:T(8,128)(2,1)}), bf16[4,24,768]{2,1,0:T(8,128)(2,1)}, u32[]{:S(2)}, u32[]{:S(2)}) async-start(bf16[4,24,768]{2,1,0:T(8,128)(2,1)} %bitcast.150), calls=%async_computation.5 | async-start | bytes 294912 | tf_op jit(solution)/shard_map/all_to_all | solution.py:325
  438.3 1.4 collective-permute-start.30
  440.4 50.2 %copy-start.16 = (f32[512,768]{1,0:T(8,128)S(1)}, f32[512,768]{1,0:T(8,128)}, u32[]{:S(2)}) copy-start(f32[512,768]{1,0:T(8,128)} %get-tuple-element.51) | copy-start | bytes 4718596
  486.0 11.0 %all-to-all-start.1 = ((bf16[4,28,576]{2,1,0:T(8,128)(2,1)}), bf16[4,28,576]{2,1,0:T(8,128)(2,1)S(1)}, u32[]{:S(2)}, u32[]{:S(2)}) async-start(bf16[4,28,576]{2,1,0:T(8,128)(2,1)} %reshape.1367), calls=%async_computation.2 | async-start | bytes 327680 | tf_op jit(solution)/shard_map/all_to_all | solution.py:325
  (59 other events, 254.8 us)
Sparse Core Ops, SparseCore 0:
  32.7 23.9 all-gather.3
  59.2 28.1 all-gather.5
  89.3 24.0 all-gather.7
  325.6 34.9 reduce-scatter.8
  364.4 40.0 reduce-scatter.6
  407.8 36.8 reduce-scatter.10
  448.0 36.2 reduce-scatter.4
